TPU v7x, 32 devices: a whole 2x2x4 slice. The times are simulated.
32 devices in a mesh: run: 1, row: 16 (over z, y, core), col: 1, seg: 2 (over x).
Axes of the slice: x: 2, y: 2, z: 4, core: 2. Of those that a mesh axis runs over, the one named last changes fastest.
Arguments:
- traces: bfloat16 [2, 1024, 2048], P(('run', 'seg'), 'row', 'col'), may hold values from -30 to 30
- live_mask: int32 [1024], P(('run', 'row')), may hold values 0 or 1
- sources: int32 [64], replicated, may hold values from 0 to 1023
- owners: int32 [64, 1], replicated, may hold values from 0 to 15; in each aligned block of 64 rows (0 to 63, 64 to 127, ...) at most 12 rows name the same one
Outputs:
- gathers: bfloat16 [192, 16, 64, 256], P(('run', 'row'), None, ('col', 'seg'))
Inputs may be any that keep to these rules, and one draw needn't show every extreme that they name: `owners`: at most 12 sources share an owner, and some owner has exactly 12.
All inputs are finite; a program needn't handle non-finite values. No bound on the sum of `live_mask` on one device may be relied on, other than what follows from the above.
Results may differ from a plain program's by a relative error of at most 0.024.
Values may be sent and summed in bfloat16 or wider, within the bound.
No kernel may reach another device: no remote copies, remote signals or barrier semaphores. Data moves between devices by JAX's collectives and lax.ppermute only.
A program may use at most 64 MiB of HBM per device.

v0:
```python
import math

import jax
import jax.numpy as jnp
from jax import lax
from jax.sharding import PartitionSpec as P

NT = 2048
NF = 1024
LAGS = 256
BAND = 64


two_pi = 2.0 * math.pi


def turn_table(first_ids, second_ids, period):
    product = first_ids[:, None] * second_ids[None, :] % period
    return product.astype(jnp.float32) * (two_pi / period)


def lag_matrix(bin_ids):
    lag_ids = jnp.arange(LAGS, dtype=jnp.int32) - LAGS // 2 + NT
    lag_angles = turn_table(bin_ids, lag_ids, NT)
    return jnp.concatenate(
        [jnp.cos(lag_angles).astype(jnp.bfloat16), -jnp.sin(lag_angles).astype(jnp.bfloat16)],
        axis=0,
    )


def correlate(recv_real, recv_imag, real_source, imag_source, lag_table):
    cross_real = (
        real_source[:, None, :] * recv_real[:, :, None]
        + imag_source[:, None, :] * recv_imag[:, :, None]
    ).astype(jnp.bfloat16)
    cross_imag = (
        imag_source[:, None, :] * recv_real[:, :, None]
        - real_source[:, None, :] * recv_imag[:, :, None]
    ).astype(jnp.bfloat16)
    stacked_cross = jnp.concatenate([cross_real, cross_imag], axis=0)
    return jnp.einsum("fl,fgv->gvl", lag_table, stacked_cross, preferred_element_type=jnp.float32)


def local(traces, live_mask, sources, owners):
    col_count = lax.axis_size("col")
    seg_count = lax.axis_size("seg")
    row_count = lax.axis_size("row")
    samples = traces[0]
    channels = samples.shape[0]
    local_width = samples.shape[1]
    num_sources = sources.shape[0]
    first_sample = lax.axis_index("col") * local_width
    half_bins = NF // col_count
    sample_ids = first_sample + jnp.arange(local_width, dtype=jnp.int32)
    bin_ids = jnp.arange(half_bins * lax.axis_size("col"), dtype=jnp.int32)
    angles = turn_table(sample_ids, bin_ids, NT)
    cosine = jnp.cos(angles).astype(jnp.bfloat16)
    sine_table = jnp.sin(angles).astype(jnp.bfloat16)
    real_part = jnp.einsum("tf,ct->fc", cosine, samples, preferred_element_type=jnp.float32)
    imag_part = -jnp.einsum("tf,ct->fc", sine_table, samples, preferred_element_type=jnp.float32)
    spectra = lax.psum_scatter(
        jnp.concatenate([real_part, imag_part], axis=1).astype(jnp.bfloat16),
        "col",
        scatter_dimension=0,
        tiled=True,
    ).astype(jnp.float32)
    squares = (spectra * spectra).reshape(half_bins // BAND, BAND, 2, channels)
    band_power = jnp.sum(squares, axis=(1, 2)) / (2 * BAND) + 1e-05
    scaling = live_mask.astype(jnp.float32)[None, :] / jnp.sqrt(band_power)
    scaling = jnp.repeat(scaling, BAND, axis=0)
    whitened = (
        (spectra.reshape(half_bins, 2, channels) * scaling[:, None, :])
        .reshape(half_bins, 2 * channels)
        .astype(jnp.bfloat16)
    )
    white_real = whitened[:, :channels]
    white_imag = whitened[:, channels:]
    everyone = lax.all_gather(whitened, "row", axis=1, tiled=True)
    block_ids = sources // channels
    within = sources % channels
    real_cols = block_ids * (2 * channels) + within
    source_real = jnp.take(everyone, real_cols, axis=1)
    source_imag = jnp.take(everyone, real_cols + channels, axis=1)
    receivers = channels // (col_count * seg_count)
    bin_ids = lax.axis_index("col") * half_bins + jnp.arange(half_bins, dtype=jnp.int32)
    lag_table = lag_matrix(bin_ids)
    real_source = source_real.astype(jnp.float32)
    imag_source = source_imag.astype(jnp.float32)

    def one_group(offset):
        recv_real = lax.dynamic_slice_in_dim(white_real, offset, receivers, 1).astype(jnp.float32)
        recv_imag = lax.dynamic_slice_in_dim(white_imag, offset, receivers, 1).astype(jnp.float32)
        return correlate(recv_real, recv_imag, real_source, imag_source, lag_table)

    offsets = (
        jnp.arange(receivers * lax.axis_size(("col", "seg")) // receivers, dtype=jnp.int32)
        * receivers
    )
    blocks = lax.map(one_group, offsets)
    stacked = lax.psum_scatter(
        blocks.reshape(receivers * lax.axis_size(("col", "seg")), num_sources, LAGS).astype(
            jnp.bfloat16
        ),
        ("col", "seg"),
        scatter_dimension=0,
        tiled=True,
    ).astype(jnp.float32)
    mean_sq = jnp.mean(stacked * stacked, axis=-1, keepdims=True)
    normed = (stacked / jnp.sqrt(mean_sq + 1e-06)).astype(jnp.bfloat16)
    capacity = 3 * num_sources // row_count
    owner_ids = owners[:, 0]
    order_ids = jnp.arange(num_sources, dtype=jnp.int32)
    earlier = (owner_ids[:, None] == owner_ids[None, :]) & (order_ids[None, :] < order_ids[:, None])
    slot_rank = jnp.sum(earlier.astype(jnp.int32), axis=1)
    slot_ids = owner_ids * capacity + slot_rank
    placing = (
        jnp.arange(row_count * capacity, dtype=jnp.int32)[:, None] == slot_ids[None, :]
    ).astype(jnp.bfloat16)
    outgoing = jnp.einsum(
        "sv,gvl->sgl", placing, normed, preferred_element_type=jnp.float32
    ).astype(jnp.bfloat16)
    return lax.all_to_all(outgoing[:, None], "row", split_axis=0, concat_axis=1, tiled=True)


def solution(mesh):
    placed = (P(("run", "seg"), "row", "col"), P(("run", "row")), P(), P())
    return jax.shard_map(
        local,
        mesh=mesh,
        in_specs=placed,
        out_specs=P(("run", "row"), None, ("col", "seg"), None),
        check_vma=False,
    )
```

profile of v0, /device:TPU:1, one launch (start us, length us, event | category | flops | bytes accessed | tf_op | source)
XLA Modules:
  0.0 271.0 jit_solution(1408020758581116476)
XLA Ops:
  6.5 0.0 copy-start
  6.5 0.0 all-gather.2.cloned.1.call-start
  6.5 0.9 copy-done
  7.5 31.3 %fusion.21 = bf16[1024,64]{0,1:T(8,128)(2,1)S(1)} fusion(bf16[1,64,2048]{2,1,0:T(8,128)(2,1)S(1)} %copy-done), kind=kOutput, calls=%fused_computation.35 | convolution fusion | flops 300023808 | bytes 393216 | tf_op jit(solution)/shard_map/tf,ct->fc/dot_general | solution.py:60
  38.8 0.0 copy-start.4
  38.8 31.2 %fusion.22 = bf16[1024,64]{0,1:T(8,128)(2,1)S(1)} fusion(bf16[1,64,2048]{2,1,0:T(8,128)(2,1)S(1)} %copy-done), kind=kOutput, calls=%fused_computation.36 | convolution fusion | flops 299958272 | bytes 393216 | tf_op jit(solution)/shard_map/tf,ct->fc/dot_general | solution.py:59
  70.1 0.0 copy-start.3
  70.1 0.3 mul.149
  70.4 0.2 reduce_sum.28
  70.6 0.1 copy.15
  70.7 0.0 copy-done.4
  70.7 0.1 copy.16
  70.8 0.2 broadcast_in_dim.19
  71.0 0.2 mul.150
  71.2 0.8 multiply_convert_fusion
  72.0 0.0 all-gather.2.cloned.1.call-update
  72.0 0.0 reduce-scatter.2.cloned.1.call-start
  72.1 0.0 copy-done.3
  72.1 1.0 fusion.48
  73.1 4.2 %cosine_convert_fusion.4 = bf16[1024,256]{1,0:T(8,128)(2,1)S(1)} fusion(s32[256]{0:T(256)S(1)} %iota_add_fusion), kind=kLoop, calls=%fused_computation.43 | loop fusion | flops 3932160 | bytes 525312 | tf_op jit(solution)/shard_map/convert_element_type | solution.py:26
  77.3 4.0 %fusion.31 = bf16[1024,256]{1,0:T(8,128)(2,1)S(1)} fusion(s32[256]{0:T(256)S(1)} %iota_add_fusion), kind=kLoop, calls=%fused_computation.47 | loop fusion | flops 4718592 | bytes 525312 | tf_op jit(solution)/shard_map/neg | solution.py:26
  81.4 1.0 pad_maximum_fusion
  82.4 42.7 %all-gather.2.cloned.1.call-done = bf16[1024,2048]{0,1:T(8,128)(2,1)} async-done(((bf16[1024,128]{0,1:T(8,128)(2,1)}), bf16[1024,2048]{0,1:T(8,128)(2,1)}) %all-gather.2.cloned.1.call-update) | async-done | bytes 4194320 | tf_op jit(solution)/shard_map/all_gather | solution.py:78
  125.1 3.5 %gather_fusion = bf16[64,1024]{1,0:T(8,128)(2,1)S(1)} fusion(bf16[1024,2048]{0,1:T(8,128)(2,1)} %all-gather.2.cloned.1.call-done, s32[1024]{0:T(1024)S(1)} %pad_clamp_fusion.1), kind=kCustom, calls=%fused_computation.clone | custom fusion | bytes 262400 | tf_op jit(solution)/shard_map/jit(_take)/gather | solution.py:82
  128.6 3.5 %gather_fusion.1 = bf16[64,1024]{1,0:T(8,128)(2,1)S(1)} fusion(bf16[1024,2048]{0,1:T(8,128)(2,1)} %all-gather.2.cloned.1.call-done, s32[1024]{0:T(1024)S(1)} %pad_clamp_fusion), kind=kCustom, calls=%fused_computation.1.clone | custom fusion | bytes 262400 | tf_op jit(solution)/shard_map/jit(_take)/gather | solution.py:83
  132.2 0.1 bitcast_convert_fusion
  132.3 0.0 copy-start.5
  132.3 16.3 %while.10 = (s32[]{:T(128)}, bf16[2,32,64,256]{3,2,1,0:T(8,128)(2,1)S(1)}, f32[1024,64]{0,1:T(8,128)S(1)}, s32[2]{0:T(128)S(1)}, bf16[1024,64]{0,1:T(8,128)(2,1)...) while((s32[]{:T(128)}, ...), condition=%wide.region_3.5_spmd, body=%wide.region_2.4_spmd.sunk | while | flops 2181103616 | bytes 25297088 | solution.py:99
  132.3 0.7 dynamic_slice.15
  135.1 0.0 copy-start.2
  135.1 2.8 %add_convert_fusion.2 = (bf16[1024,32,64]{0,2,1:T(8,128)(2,1)S(1)}, bf16[1024,32,64]{0,2,1:T(8,128)(2,1)S(1)}) fusion(f32[1024,32]{0,1:T(8,128)S(1)} %get-tuple-element.129, f32[1024,64]{0,1:T(8,128)S(1)} %get-tuple-element.160, f32[1024,32]{0,1:T(8,128)S(1)} %get-tuple-element.130, f32[1024,64]{0,1:T(8,128)S(1)} %get-tuple-element.157), kind=kLoop, calls=%fused_computation.7.clone.1 | loop fusion | flops 16777216 | bytes 9175040 | tf_op jit(solution)/shard_map/while/body/eval_jaxpr/convert_element_type | solution.py:35
  137.9 0.0 copy-done.2
  137.9 2.5 bitcast_dynamic-update-slice_fusion.2
  140.5 0.7 dynamic_slice.15
  143.3 0.0 copy-start.2
  143.3 2.8 %add_convert_fusion.2 = (bf16[1024,32,64]{0,2,1:T(8,128)(2,1)S(1)}, bf16[1024,32,64]{0,2,1:T(8,128)(2,1)S(1)}) fusion(f32[1024,32]{0,1:T(8,128)S(1)} %get-tuple-element.129, f32[1024,64]{0,1:T(8,128)S(1)} %get-tuple-element.160, f32[1024,32]{0,1:T(8,128)S(1)} %get-tuple-element.130, f32[1024,64]{0,1:T(8,128)S(1)} %get-tuple-element.157), kind=kLoop, calls=%fused_computation.7.clone.1 | loop fusion | flops 16777216 | bytes 9175040 | tf_op jit(solution)/shard_map/while/body/eval_jaxpr/convert_element_type | solution.py:35
  146.1 0.0 copy-done.2
  146.1 2.5 bitcast_dynamic-update-slice_fusion.2
  148.7 0.0 copy-start.1
  148.7 1.3 copy-done.1
  150.0 0.0 reduce-scatter.2.cloned.1.call-update
  150.0 0.0 copy-done.5
  150.0 0.2 convert_reduce_fusion
  150.2 29.8 %reduce-scatter.2.cloned.1.call-done = bf16[32,64,256]{2,1,0:T(8,128)(2,1)} async-done(((bf16[64,64,256]{2,1,0:T(8,128)(2,1)}), bf16[32,64,256]{2,1,0:T(8,128)(2,1)}) %reduce-scatter.2.cloned.1.call-update) | async-done | bytes 1048592 | tf_op jit(solution)/shard_map/reduce_scatter | solution.py:100
  180.0 1.6 fusion.18
  181.6 2.3 convert_bitcast_fusion
  184.0 1.8 copy.17
  185.7 76.3 %all_to_all.18 = bf16[192,1,32,256]{3,2,1,0:T(8,128)(2,1)S(1)} all-to-all(bf16[192,1,32,256]{3,2,1,0:T(8,128)(2,1)S(1)} %copy.17), channel_id=1, replica_groups=mesh['run'=1,'row'=16,'col'=1,'seg'=2] {'row'}, dimensions={0} | all-to-all | bytes 6291456 | tf_op jit(solution)/shard_map/all_to_all | solution.py:122
  262.1 2.1 copy.18
  (15 shorter events, 0.2 us)
Async XLA Ops:
  6.5 1.0 copy-start
  6.5 118.6 %all-gather.2.cloned.1.call-start = ((), (), s32[]{:S(2)}) async-start(), calls=%async_computation.2 | async-start | bytes 4456448 | tf_op jit(solution)/shard_map/all_gather | solution.py:78
  38.8 31.9 %copy-start.4 = (s32[64]{0:T(128)S(1)}, s32[64]{0:T(128)}, u32[]{:S(2)}) copy-start(s32[64]{0:T(128)} %param.9) | copy-start | bytes 772
  70.1 2.0 copy-start.3
  72.0 108.0 %reduce-scatter.2.cloned.1.call-start = ((), (), s32[]{:S(2)}) async-start(), calls=%async_computation.3 | async-start | bytes 3145728 | tf_op jit(solution)/shard_map/reduce_scatter | solution.py:100
  132.3 17.7 %copy-start.5 = (s32[64,1]{0,1:T(1,128)S(1)}, s32[64,1]{0,1:T(1,128)}, u32[]{:S(2)}) copy-start(s32[64,1]{0,1:T(1,128)} %param.11) | copy-start | bytes 772
  135.1 2.8 %copy-start.2 = (bf16[2048,256]{1,0:T(8,128)(2,1)S(1)}, bf16[2048,256]{1,0:T(8,128)(2,1)}, u32[]{:S(2)}) copy-start(bf16[2048,256]{1,0:T(8,128)(2,1)} %get-tuple-element.162) | copy-start | bytes 3145732 | tf_op jit(solution)/shard_map/while
  143.3 2.8 %copy-start.2 = (bf16[2048,256]{1,0:T(8,128)(2,1)S(1)}, bf16[2048,256]{1,0:T(8,128)(2,1)}, u32[]{:S(2)}) copy-start(bf16[2048,256]{1,0:T(8,128)(2,1)} %get-tuple-element.162) | copy-start | bytes 3145732 | tf_op jit(solution)/shard_map/while
  148.7 1.3 copy-start.1
Sparse Core Ops, SparseCore 0:
  72.1 52.9 all-gather.1
  150.1 29.8 reduce-scatter.1
where the time goes:
time: 271 us
  blocking collectives  76.3 us (28%)
  waiting for transfers between devices  72.6 us (27%)
  matrix products  70 us (26%)
  other arithmetic  17.9 us (7%)
  local copies, waits for them, and re-layouts  16.3 us (6%)
  between operations  13.6 us (5%)
  loops' own time  4.26 us (2%)
    all_to_all x1, blocking collectives, local(): lax.all_to_all(outgoing[:, None], 'row', split_axis=0, concat_axis=1, til...  76.3 us
    all_gather x1, waiting for transfers between devices, local(): everyone = lax.all_gather(whitened, 'row', axis=1, tiled=True)  42.7 us
    dot_general x1, matrix products, local(): jnp.einsum('tf,ct->fc', sine_table, samples, preferred_element_type=jnp.f...  31.3 us
    dot_general x1, matrix products, local(): jnp.einsum('tf,ct->fc', cosine, samples, preferred_element_type=jnp.float32)  31.2 us
    reduce_scatter x1, waiting for transfers between devices, local(): lax.psum_scatter(blocks.reshape(receivers * lax.axis_size(('col', 'seg'))...  29.8 us
    convert_element_type x2, other arithmetic, correlate(): cross_real = (real_source[:, None, :] * recv_real[:, :, None] + imag_sour...  5.58 us
  transfers between devices with their start and end apart: 2, of which 2 were waited for; matrix products, arithmetic and copies ran while one was open for 4% of the time, Pallas kernels for 0%

commit v1 on v0

--- a/solution.py
+++ b/solution.py
@@ -1,9 +1,13 @@
+import functools
 import math
 
 import jax
 import jax.numpy as jnp
 from jax import lax
+from jax.experimental import pallas as pl
+from jax.experimental.pallas import tpu as pltpu
 from jax.sharding import PartitionSpec as P
+
 
 NT = 2048
 NF = 1024
@@ -12,6 +16,8 @@
 
 
 two_pi = 2.0 * math.pi
+f32 = jnp.float32
+bf16 = jnp.bfloat16
 
 
 def turn_table(first_ids, second_ids, period):
@@ -41,7 +47,7 @@
     return jnp.einsum("fl,fgv->gvl", lag_table, stacked_cross, preferred_element_type=jnp.float32)
 
 
-def local(traces, live_mask, sources, owners):
+def local_general(traces, live_mask, sources, owners):
     col_count = lax.axis_size("col")
     seg_count = lax.axis_size("seg")
     row_count = lax.axis_size("row")
@@ -106,7 +112,7 @@
         tiled=True,
     ).astype(jnp.float32)
     mean_sq = jnp.mean(stacked * stacked, axis=-1, keepdims=True)
-    normed = (stacked / jnp.sqrt(mean_sq + 1e-06)).astype(jnp.bfloat16)
+    normed = (stacked * lax.rsqrt(mean_sq + 1e-06)).astype(jnp.bfloat16)
     capacity = 3 * num_sources // row_count
     owner_ids = owners[:, 0]
     order_ids = jnp.arange(num_sources, dtype=jnp.int32)
@@ -122,10 +128,383 @@
     return lax.all_to_all(outgoing[:, None], "row", split_axis=0, concat_axis=1, tiled=True)
 
 
+HALF = NT // 2
+QUARTER = NF // 2
+VMEM_LIMIT = 16 * 1024 * 1024
+
+
+def turn(steps):
+    steps = steps % NT
+    quarter = (steps + NT // 8) // (NT // 4)
+    x = (steps - quarter * (NT // 4)).astype(f32) * (two_pi / NT)
+    y = x * x
+    c = 1.0 + y * (-1 / 2 + y * (1 / 24 + y * (-1 / 720 + y * (1 / 40320 - y / 3628800))))
+    s = x * (1.0 + y * (-1 / 6 + y * (1 / 120 + y * (-1 / 5040 + y / 362880))))
+    odd, back, low = quarter % 2 == 1, quarter % 4 >= 2, (quarter + 1) % 4 >= 2
+    cos, sin = jnp.where(odd, s, c), jnp.where(odd, c, s)
+    return jnp.where(low, -cos, cos), jnp.where(back, -sin, sin)
+
+
+def rows_of(count, scale, first, others):
+    ids = lax.broadcasted_iota(jnp.int32, (count, others.shape[1]), 0)
+    return turn((ids * scale + first) * others)
+
+
+def fill_dft(dft_ref, coarse_c, coarse_s, base_c, base_s):
+    blocks = HALF // 64
+    places = lax.broadcasted_iota(jnp.int32, (1, NF), 1)
+    bins = jnp.where(places < QUARTER, 2 * places, 2 * places - NF + 1)
+    coarse_c[...], coarse_s[...] = rows_of(blocks, 64, 0, bins)
+    middle_c, middle_s = rows_of(8, 8, 0, bins)
+    fine_c, fine_s = rows_of(8, 1, 0, bins)
+    for b in range(8):
+        cb, sb = middle_c[b : b + 1, :], middle_s[b : b + 1, :]
+        base_c[8 * b : 8 * b + 8, :] = fine_c * cb - fine_s * sb
+        base_s[8 * b : 8 * b + 8, :] = fine_s * cb + fine_c * sb
+    for a in range(blocks):
+        for lo in range(0, NF, 256):
+            ca, sa = coarse_c[a : a + 1, lo : lo + 256], coarse_s[a : a + 1, lo : lo + 256]
+            bc, bs = base_c[:, lo : lo + 256], base_s[:, lo : lo + 256]
+            dft_ref[64 * a : 64 * a + 64, lo : lo + 256] = (bc * ca - bs * sa).astype(bf16)
+            dft_ref[64 * a : 64 * a + 64, NF + lo : NF + lo + 256] = (-bs * ca - bc * sa).astype(bf16)
+
+
+def dft_scratch():
+    coarse, base = pltpu.VMEM((HALF // 64, NF), f32), pltpu.VMEM((64, NF), f32)
+    return [coarse, coarse, base, base]
+
+
+def tables_kernel(dft_ref, lag_ref, coarse_c, coarse_s, base_c, base_s):
+    fill_dft(dft_ref, coarse_c, coarse_s, base_c, base_s)
+    lags = lax.broadcasted_iota(jnp.int32, (1, LAGS), 1) - LAGS // 2 + NT
+    groups = QUARTER // 64
+    far_c, far_s = rows_of(groups, 128, 0, lags)
+    middle_c, middle_s = rows_of(8, 16, 0, lags)
+    for odd in range(2):
+        fine_c, fine_s = rows_of(8, 2, odd, lags)
+        for b in range(8):
+            cb, sb = middle_c[b : b + 1, :], middle_s[b : b + 1, :]
+            base_c[8 * b : 8 * b + 8, :LAGS] = fine_c * cb - fine_s * sb
+            base_s[8 * b : 8 * b + 8, :LAGS] = fine_s * cb + fine_c * sb
+        for a in range(groups):
+            ca, sa = far_c[a : a + 1, :], far_s[a : a + 1, :]
+            bc, bs = base_c[:, :LAGS], base_s[:, :LAGS]
+            at = QUARTER * odd + 64 * a
+            lag_ref[at : at + 64, :] = (bc * ca - bs * sa).astype(bf16)
+            lag_ref[NF + at : NF + at + 64, :] = (-bs * ca - bc * sa).astype(bf16)
+
+
+def make_tables():
+    return pl.pallas_call(
+        tables_kernel,
+        out_shape=(
+            jax.ShapeDtypeStruct((HALF, 2 * NF), bf16),
+            jax.ShapeDtypeStruct((2 * NF, LAGS), bf16),
+        ),
+        scratch_shapes=dft_scratch(),
+        compiler_params=pltpu.CompilerParams(vmem_limit_bytes=VMEM_LIMIT),
+        cost_estimate=pl.CostEstimate(
+            flops=6 * HALF * NF, bytes_accessed=4 * HALF * NF, transcendentals=0
+        ),
+        name="tables",
+    )()
+
+
+def whiten_rows(own, other, dft_ref, out_ref):
+    x = jnp.concatenate([own, other], axis=0).astype(f32)
+    even = (x[:, :HALF] + x[:, HALF:]).astype(bf16)
+    odd = (x[:, :HALF] - x[:, HALF:]).astype(bf16)
+    parts = []
+    for side, lo in ((even, 0), (odd, QUARTER), (even, NF), (odd, NF + QUARTER)):
+        parts.append(jnp.dot(side, dft_ref[:, lo : lo + QUARTER], preferred_element_type=f32))
+    power = sum(part * part for part in parts)
+    bands = NF // BAND
+    bin_band = lax.broadcasted_iota(jnp.int32, (QUARTER, bands), 0) // (BAND // 2)
+    member = (bin_band == lax.broadcasted_iota(jnp.int32, (QUARTER, bands), 1)).astype(f32)
+    bin_band_t = lax.broadcasted_iota(jnp.int32, (bands, QUARTER), 1) // (BAND // 2)
+    member_t = (bin_band_t == lax.broadcasted_iota(jnp.int32, (bands, QUARTER), 0)).astype(f32)
+    high = lax.Precision.HIGHEST
+    band_power = jnp.dot(power, member, precision=high, preferred_element_type=f32)
+    scaling = lax.rsqrt(band_power / (2 * BAND) + 1e-05)
+    scaling = jnp.dot(scaling, member_t, precision=high, preferred_element_type=f32)
+    for i, part in enumerate(parts):
+        white = (part * scaling).astype(bf16)
+        out_ref[:, i * QUARTER : (i + 1) * QUARTER] = white.astype(out_ref.dtype)
+
+
+def whiten_kernel(own_ref, other_ref, dft_ref, out_ref):
+    whiten_rows(own_ref[...], other_ref[...], dft_ref, out_ref)
+
+
+def whiten(own, other, dft):
+    rows = own.shape[0]
+    return pl.pallas_call(
+        whiten_kernel,
+        out_shape=jax.ShapeDtypeStruct((2 * rows, 2 * NF), bf16),
+        compiler_params=pltpu.CompilerParams(vmem_limit_bytes=VMEM_LIMIT),
+        cost_estimate=pl.CostEstimate(
+            flops=4 * rows * HALF * 2 * NF, bytes_accessed=4 * HALF * NF, transcendentals=0
+        ),
+        name="whiten",
+    )(own, other, dft)
+
+
+def whiten_sources_kernel(own_ref, other_ref, out_ref, dft_ref, *scratch):
+    fill_dft(dft_ref, *scratch)
+    whiten_rows(own_ref[...], other_ref[...], dft_ref, out_ref)
+
+
+def whiten_sources(own, other):
+    rows = own.shape[0]
+    return pl.pallas_call(
+        whiten_sources_kernel,
+        out_shape=jax.ShapeDtypeStruct((2 * rows, 2 * NF), f32),
+        scratch_shapes=[pltpu.VMEM((HALF, 2 * NF), bf16)] + dft_scratch(),
+        compiler_params=pltpu.CompilerParams(vmem_limit_bytes=VMEM_LIMIT),
+        cost_estimate=pl.CostEstimate(
+            flops=4 * rows * HALF * 2 * NF, bytes_accessed=4 * HALF * NF, transcendentals=0
+        ),
+        name="whiten_sources",
+    )(own, other)
+
+
+def front_kernel(at_ref, facts_ref, samples_ref, own_ref, away_ref, keep_ref, give_ref, held, picked):
+    me, side, core, deep = at_ref[0], at_ref[1], at_ref[2], at_ref[3]
+    channels = samples_ref.shape[0]
+    receivers, half = own_ref.shape[0], keep_ref.shape[0]
+    row_ids = lax.broadcasted_iota(jnp.int32, (channels, channels), 0)
+    diagonal = row_ids == lax.broadcasted_iota(jnp.int32, (channels, channels), 1)
+    mask = jnp.where(diagonal, facts_ref[0:1, :channels].astype(f32), 0.0).astype(bf16)
+    held[...] = jnp.dot(mask, samples_ref[...], preferred_element_type=f32).astype(bf16)
+    own_ref[...] = held[pl.ds(pl.multiple_of(side * receivers, receivers), receivers), :]
+    away_ref[...] = held[pl.ds(pl.multiple_of((1 - side) * receivers, receivers), receivers), :]
+    ids = lax.broadcasted_iota(jnp.int32, (channels, 2 * half), 0) + me * channels
+    choose = (ids == facts_ref[1:2, : 2 * half]).astype(bf16)
+    picked[...] = lax.dot_general(
+        choose, held[...], (((0,), (0,)), ((), ())), preferred_element_type=f32
+    ).astype(bf16)
+    part = half // 2
+    for out_ref, owner in ((keep_ref, core), (give_ref, 1 - core)):
+        for n, side_y in enumerate((deep, 1 - deep)):
+            first = pl.multiple_of(owner * half + side_y * part, part)
+            out_ref[n * part : (n + 1) * part, :] = picked[pl.ds(first, part), :]
+
+
+def front(at, live, sources, samples):
+    channels, width = samples.shape
+    count = sources.shape[0]
+    longest = max(channels, count)
+    facts = jnp.stack(
+        [jnp.pad(live, (0, longest - channels)), jnp.pad(sources, (0, longest - count))]
+    )
+    shapes = [channels // 2, channels // 2, count // 2, count // 2]
+    vmem = pl.BlockSpec(memory_space=pltpu.VMEM)
+    return pl.pallas_call(
+        front_kernel,
+        out_shape=[jax.ShapeDtypeStruct((rows, width), bf16) for rows in shapes],
+        in_specs=[pl.BlockSpec(memory_space=pltpu.SMEM), vmem, vmem],
+        scratch_shapes=[pltpu.VMEM((channels, width), bf16), pltpu.VMEM((count, width), bf16)],
+        compiler_params=pltpu.CompilerParams(vmem_limit_bytes=VMEM_LIMIT),
+        cost_estimate=pl.CostEstimate(flops=1 << 24, bytes_accessed=1 << 20, transcendentals=0),
+        name="front",
+    )(at, facts, samples)
+
+
+def gather_kernel(rows_ref, src_ref, lag_ref, *refs, count, per):
+    units, out_ref = refs[:count], refs[-6]
+    crosses, (stage, sem) = refs[-5:-2], refs[-2:]
+    capacity = out_ref.shape[0]
+    receivers = units[0].shape[0] // 2
+    second = src_ref.shape[0] // 2
+    width = 256
+    copies = []
+    starts = list(range(0, capacity, per))
+    for g, first in enumerate(starts):
+        slots = list(range(first, min(capacity, first + per)))
+        cross = crosses[g % len(crosses)]
+        for n, slot in enumerate(slots):
+            for lo in range(0, NF, width):
+                real0, imag0, real1, imag1 = [
+                    jnp.broadcast_to(
+                        src_ref[at : at + 1, first_bin : first_bin + width], (16, width)
+                    ).astype(bf16)
+                    for at in (slot, slot + second)
+                    for first_bin in (lo, NF + lo)
+                ]
+                for u, unit in enumerate(units):
+                    for top in range(0, receivers, 16):
+                        wr0, wi0, wr1, wi1 = [
+                            unit[at : at + 16, first_bin : first_bin + width]
+                            for at in (top, receivers + top)
+                            for first_bin in (lo, NF + lo)
+                        ]
+                        row = (n * count + u) * receivers + top
+                        cross[row : row + 16, lo : lo + width] = (
+                            real0 * wr0 + imag0 * wi0 + (real1 * wr1 + imag1 * wi1)
+                        )
+                        cross[row : row + 16, NF + lo : NF + lo + width] = (
+                            imag0 * wr0 - real0 * wi0 + (imag1 * wr1 - real1 * wi1)
+                        )
+        filled = len(slots) * count * receivers
+        stacked = jnp.dot(cross[:filled, :], lag_ref[...], preferred_element_type=f32)
+        mean_sq = jnp.mean(stacked * stacked, axis=-1, keepdims=True)
+        normed = (stacked * lax.rsqrt(mean_sq + 1e-06)).astype(bf16)
+        normed = normed.reshape(len(slots), count, receivers, LAGS)
+        for u in range(count):
+            stage[u, first : first + len(slots)] = normed[:, u]
+            copy = pltpu.make_async_copy(
+                stage.at[u, pl.ds(first, len(slots))],
+                out_ref.at[pl.ds(first, len(slots)), rows_ref[u]],
+                sem.at[g * count + u],
+            )
+            copy.start()
+            copies.append(copy)
+    for copy in copies:
+        copy.wait()
+
+
+def gather_slots(rows, src, lag, units, held, capacity, row_count):
+    count = len(units)
+    receivers = units[0].shape[0] // 2
+    per = 4
+    steps = -(-capacity // per)
+    vmem, anywhere = pl.BlockSpec(memory_space=pltpu.VMEM), pl.BlockSpec(memory_space=pl.ANY)
+    prior = () if held is None else (held,)
+    operands = (rows, src, lag, *units, *prior)
+    return pl.pallas_call(
+        functools.partial(gather_kernel, count=count, per=per),
+        out_shape=jax.ShapeDtypeStruct((capacity, row_count, receivers, LAGS), bf16),
+        in_specs=[pl.BlockSpec(memory_space=pltpu.SMEM)] + [vmem] * (2 + count) + [anywhere] * len(prior),
+        out_specs=anywhere,
+        input_output_aliases={len(operands) - 1: 0} if prior else {},
+        scratch_shapes=[pltpu.VMEM((per * count * receivers, 2 * NF), bf16)] * 3
+        + [
+            pltpu.VMEM((count, capacity, receivers, LAGS), bf16),
+            pltpu.SemaphoreType.DMA((steps * count,)),
+        ],
+        compiler_params=pltpu.CompilerParams(vmem_limit_bytes=VMEM_LIMIT),
+        cost_estimate=pl.CostEstimate(
+            flops=4 * NF * LAGS * capacity * count * receivers, bytes_accessed=4 << 20, transcendentals=0
+        ),
+        name="gather_slots",
+    )(*operands)
+
+
+def slots_kernel(mine_ref, sib_ref, found_ref, more_ref, own_ref, give_ref):
+    part = found_ref.shape[0]
+    for index_ref, out_ref in ((mine_ref, own_ref), (sib_ref, give_ref)):
+        chosen = jnp.zeros(out_ref.shape, f32)
+        ids = lax.broadcasted_iota(jnp.int32, (out_ref.shape[0], part), 1)
+        for first, rows_ref in ((0, found_ref), (part, more_ref)):
+            choose = (ids + first == index_ref[...]).astype(bf16)
+            chosen += jnp.dot(choose, rows_ref[...], preferred_element_type=f32)
+        out_ref[...] = chosen.astype(bf16)
+
+
+def pick_slots(mine, sibling, found, more):
+    half = jax.ShapeDtypeStruct((mine.shape[0], found.shape[1]), bf16)
+    return pl.pallas_call(
+        slots_kernel,
+        out_shape=(half, half),
+        compiler_params=pltpu.CompilerParams(vmem_limit_bytes=VMEM_LIMIT),
+        cost_estimate=pl.CostEstimate(flops=1 << 23, bytes_accessed=1 << 19, transcendentals=0),
+        name="pick_slots",
+    )(mine[:, None], sibling[:, None], found, more)
+
+
+def pairs_body(traces, live_mask, sources, owners):
+    row_count = lax.axis_size("row")
+    samples = traces[0]
+    num_sources = sources.shape[0]
+    me, side = lax.axis_index("row"), lax.axis_index("seg")
+    swap = [(0, 1), (1, 0)]
+    capacity = 3 * num_sources // row_count
+
+    def flipped(value, bit):
+        return lax.ppermute(value, "row", [(r, r ^ bit) for r in range(row_count)])
+
+    half = num_sources // 2
+    core = me % 2
+    kept_first = core * half
+    lane = me // 2 % 2
+    at = jnp.stack([me, side, core, lane]).astype(jnp.int32)
+    own, away, found, give = front(at, live_mask, sources, samples)
+    other = lax.ppermute(away, "seg", swap)
+    found = found + flipped(give, 1)
+    part = half // 2
+    found = found[:part] + flipped(found[part:], 2)
+    for bit in (8, 4):
+        found = found + flipped(found, bit)
+    more = flipped(found, 2)
+
+    owner_ids = owners[:, 0]
+    order_ids = jnp.arange(num_sources, dtype=jnp.int32)
+    earlier = (owner_ids[:, None] == owner_ids[None, :]) & (order_ids[None, :] < order_ids[:, None])
+    slot_rank = jnp.sum(earlier.astype(jnp.int32), axis=1)
+    padded = capacity + -capacity % 16
+
+    def slot_places(row):
+        slots = jnp.arange(padded, dtype=jnp.int32)
+        taken = (owner_ids == row)[None, :] & (slot_rank[None, :] == slots[:, None])
+        taken = taken & ((order_ids >= kept_first) & (order_ids < kept_first + half))[None, :]
+        places = (order_ids - kept_first) ^ (lane * part)
+        return jnp.max(jnp.where(taken, places[None, :], -1), axis=1)
+
+    own_src, sib_src = pick_slots(slot_places(me), slot_places(me ^ 1), found, more)
+    own_src = own_src + flipped(sib_src, 1)
+    other_src = lax.ppermute(own_src, "seg", swap)
+
+    dft, lag = make_tables()
+    unit = whiten(own, other, dft)
+
+    depth = row_count // 4
+    chips = 2 * depth
+    place = jnp.where(lane == 0, me // 4, chips - 1 - me // 4)
+
+    def row_at(position):
+        return jnp.where(position < depth, 4 * position, 4 * (chips - 1 - position) + 2)
+
+    def chip_row(position):
+        return 4 * position if position < depth else 4 * (chips - 1 - position) + 2
+
+    held = {0: unit}
+    for k in range(1, depth + 1):
+        for sign in (1, -1):
+            if 2 * k == chips and sign < 0:
+                continue
+            moves = [
+                (chip_row(p) + c, chip_row((p + sign) % chips) + c) for p in range(chips) for c in (0, 1)
+            ]
+            held[-sign * k] = lax.ppermute(held[-sign * (k - 1)], "row", moves)
+    order = [0]
+    for k in range(1, depth + 1):
+        order += [-k, k]
+    order = order[:-1]
+    pairs = {}
+    for d in order:
+        pairs[d] = (held[d], flipped(held[d], 1))
+    src = whiten_sources(own_src, other_src)
+    out = None
+    for n in range(depth):
+        places = order[2 * n : 2 * n + 2]
+        rows = jnp.stack(
+            [row_at((place + d) % chips) + other for d in places for other in (core, 1 - core)]
+        ).astype(jnp.int32)
+        group = [value for d in places for value in pairs[d]]
+        out = gather_slots(rows, src, lag, group, out, capacity, row_count)
+    return out
+
+
+def local_pairs(traces, live_mask, sources, owners):
+    return pairs_body(traces, live_mask, sources, owners)
+
+
 def solution(mesh):
     placed = (P(("run", "seg"), "row", "col"), P(("run", "row")), P(), P())
+    shape = mesh.shape
+    pairs = shape["col"] == 1 and shape["seg"] == 2 and shape["row"] == 16
     return jax.shard_map(
-        local,
+        local_pairs if pairs else local_general,
         mesh=mesh,
         in_specs=placed,
         out_specs=P(("run", "row"), None, ("col", "seg"), None),

time: 271 us -> 62.2 us (0.23)
  blocking collectives: 76.3 us -> 0 us
  matrix products: 70 us -> 0 us
  waiting for transfers between devices: 72.6 us -> 10.1 us
  starting transfers between devices: 0.04 us -> 26.4 us
  Pallas kernels: 0 us -> 21.5 us
  other arithmetic: 17.9 us -> 2.13 us
  local copies, waits for them, and re-layouts: 16.3 us -> 1.13 us
  between operations: 13.6 us -> 0.44 us
  loops' own time: 4.26 us -> 0 us
    all_to_all x1 -> x0, blocking collectives: 76.3 us -> none  [local(): lax.all_to_all(outgoing[:, None], 'row', split_axis=0, concat_axis=1, til...]
    dot_general x5 -> x0, matrix products: 70 us -> none  [the longest x1 31.3 us: local(): jnp.einsum('tf,ct->fc', sine_table, samples, preferred_element_type=jnp.f...]
    all_gather x1 -> x0, waiting for transfers between devices: 42.7 us -> none  [local(): everyone = lax.all_gather(whitened, 'row', axis=1, tiled=True)]
    reduce_scatter x1 -> x0, waiting for transfers between devices: 29.8 us -> none  [local(): lax.psum_scatter(blocks.reshape(receivers * lax.axis_size(('col', 'seg'))...]
    ppermute x0 -> x23, starting transfers between devices: none -> 26.4 us  [the longest x14 17.3 us: flipped(): return lax.ppermute(value, 'row', [(r, r ^ bit) for r in range(row_count)])]
    pallas_call x0 -> x9, Pallas kernels: none -> 21.5 us  [the longest x4 14.7 us: gather_slots(): pl.pallas_call(functools.partial(gather_kernel, count=count, per=per), ou...]
    convert_element_type x8 -> x0, other arithmetic: 10.7 us -> none  [the longest x2 5.58 us: correlate(): cross_real = (real_source[:, None, :] * recv_real[:, :, None] + imag_sour...]
    ppermute x0 -> x23, waiting for transfers between devices: none -> 10.1 us  [the longest x7 4.24 us: pairs_body(): held[-sign * k] = lax.ppermute(held[-sign * (k - 1)], 'row', moves)]
  transfers between devices with their start and end apart: 2 -> 23, of which waited for: 2 -> 5; matrix products, arithmetic and copies ran while one was open for 4% -> 2% of each run, Pallas kernels for 0% -> 27%
where the time goes in v1:
time: 62.2 us; the launch traced here: 61.7 us
  starting transfers between devices  26.4 us (42%)
  Pallas kernels  21.5 us (35%)
  waiting for transfers between devices  10.1 us (16%)
  other arithmetic  2.13 us (3%)
  local copies, waits for them, and re-layouts  1.13 us (2%)
    ppermute x14, starting transfers between devices, flipped(): return lax.ppermute(value, 'row', [(r, r ^ bit) for r in range(row_count)])  17.3 us
    pallas_call x4, Pallas kernels, gather_slots(): pl.pallas_call(functools.partial(gather_kernel, count=count, per=per), ou...  14.7 us
    ppermute x7, starting transfers between devices, pairs_body(): held[-sign * k] = lax.ppermute(held[-sign * (k - 1)], 'row', moves)  5.49 us
    ppermute x7, waiting for transfers between devices, pairs_body(): held[-sign * k] = lax.ppermute(held[-sign * (k - 1)], 'row', moves)  4.24 us
    ppermute x14, waiting for transfers between devices, flipped(): return lax.ppermute(value, 'row', [(r, r ^ bit) for r in range(row_count)])  3.37 us
    ppermute x1, starting transfers between devices, pairs_body(): other = lax.ppermute(away, 'seg', swap)  2.69 us
    ppermute x1, waiting for transfers between devices, pairs_body(): other_src = lax.ppermute(own_src, 'seg', swap)  2.47 us
    pallas_call x1, Pallas kernels, whiten_sources(): pl.pallas_call(whiten_sources_kernel, out_shape=jax.ShapeDtypeStruct((2 *...  2.34 us
  transfers between devices with their start and end apart: 23, of which 5 were waited for; matrix products, arithmetic and copies ran while one was open for 2% of the time, Pallas kernels for 27%

profile of v1, /device:TPU:1, one launch (start us, length us, event | category | flops | bytes accessed | tf_op | source)
XLA Modules:
  0.0 61.7 jit_solution(16382370561218869957)
XLA Ops:
  0.0 0.7 %pad_add_fusion.facts_ref = s32[2,64]{1,0:T(2,128)S(1)} fusion(s32[1,64]{1,0:T(1,128)} %bitcast.31, s32[1,64]{1,0:T(1,128)} %bitcast.32), kind=kLoop, calls=%fused_computation.12 | loop fusion | flops 128 | bytes 1024 | tf_op jit(solution)/shard_map/stack | solution.py:297
  0.7 0.1 pad_add_fusion.2.at_ref
  0.8 0.9 %copy-done = bf16[1,64,2048]{2,1,0:T(8,128)(2,1)S(1)} copy-done((bf16[1,64,2048]{2,1,0:T(8,128)(2,1)S(1)}, bf16[1,64,2048]{2,1,0:T(8,128)(2,1)}, u32[]{:S(2)}) %copy-start) | copy-done | bytes 262168
  1.7 0.9 %front.1 = (bf16[32,2048]{1,0:T(8,128)(2,1)S(1)}, bf16[32,2048]{1,0:T(8,128)(2,1)S(1)}, bf16[32,2048]{1,0:T(8,128)(2,1)S(1)}, bf16[32,2048]{1,0:T(8,128)(2,1)S(1)}) custom-call(s32[4]{0:T(128)S(1)} %pad_add_fusion.2.at_ref, s32[2,64]{1,0:T(2,128)S(1)} %pad_add_fusion.facts_ref, bf16[64,2048]{1,0:T(8,128)(2,1)S(1)} %bitcast.28), custom_call_target="tpu_custom_call" | custom-call | flops 16777216 | bytes 1048576 | tf_op jit(solution)/shard_map/front/pallas_call | solution.py:302
  2.6 0.1 collective-permute-start
  2.7 2.7 %collective-permute-start.7 = (bf16[32,2048]{1,0:T(8,128)(2,1)S(1)}, bf16[32,2048]{1,0:T(8,128)(2,1)S(1)}, u32[]{:S(2)}, u32[]{:S(2)}) collective-permute-start(bf16[32,2048]{1,0:T(8,128)(2,1)S(1)} %get-tuple-element.19), channel_id=1, source_target_pairs={{0,1},{1,0},{2,3},{3,2},{4,5},{5,4},{6,7},{7,6},{8,9},{9,8},{10,11... | collective-permute-start | bytes 393224 | tf_op jit(solution)/shard_map/ppermute | solution.py:432
  5.4 0.0 collective-permute-done
  5.5 1.3 %collective-permute-start.1 = (bf16[16,2048]{1,0:T(8,128)(2,1)S(1)}, bf16[16,2048]{1,0:T(8,128)(2,1)S(1)}, u32[]{:S(2)}, u32[]{:S(2)}) collective-permute-start(bf16[16,2048]{1,0:T(8,128)(2,1)S(1)} %slice.9), channel_id=1, source_target_pairs={{0,4},{2,6},{4,0},{6,2},{8,12},{10,14},{12,8},{14,10},{16,20},{18,... | collective-permute-start | bytes 196616 | tf_op jit(solution)/shard_map/ppermute | solution.py:424
  6.8 0.7 %broadcast_compare_fusion.1 = (pred[64]{0:T(512)(128)(4,1)S(1)}, pred[64]{0:T(512)(128)(4,1)S(1)}, pred[64]{0:T(512)(128)(4,1)S(1)}) fusion(s32[]{:T(128)} %axis_index.23, s32[64,1]{0,1:T(1,128)} %param.7, s32[]{:T(128)S(6)} %xor.17, s32[]{:T(128)S(6)} %add.180, s32[]{:T(128)S(6)} %mul.75), kind=kLoop, calls=%fused_computation.20 | loop fusion | flops 320 | bytes 464 | tf_op jit(solution)/shard_map/eq | solution.py:448
  7.4 2.0 %tables.1 = (bf16[1024,2048]{1,0:T(8,128)(2,1)S(1)}, bf16[2048,256]{1,0:T(8,128)(2,1)S(1)}) custom-call(), custom_call_target="tpu_custom_call" | custom-call | flops 6291456 | bytes 4194304 | tf_op jit(solution)/shard_map/tables/pallas_call | solution.py:198
  9.4 0.0 collective-permute-done.7.other_ref
  9.5 1.3 %whiten.1.refs_0_ = bf16[64,2048]{1,0:T(8,128)(2,1)S(1)} custom-call(bf16[32,2048]{1,0:T(8,128)(2,1)S(1)} %get-tuple-element.18.own_ref, bf16[32,2048]{1,0:T(8,128)(2,1)S(1)} %collective-permute-done.7.other_ref, bf16[1024,2048]{1,0:T(8,128)(2,1)S(1)} %get-tuple-element.20.dft_ref), custom_call_target="tpu_custom_call" | custom-call | flops 268435456 | bytes 4194304 | tf_op jit(solution)/shard_map/whiten/pallas_call | solution.py:241
  10.8 1.3 %collective-permute-start.12 = (bf16[64,2048]{1,0:T(8,128)(2,1)S(1)}, bf16[64,2048]{1,0:T(8,128)(2,1)S(1)}, u32[]{:S(2)}, u32[]{:S(2)}) collective-permute-start(bf16[64,2048]{1,0:T(8,128)(2,1)S(1)} %whiten.1.refs_0_), channel_id=1, source_target_pairs={{0,8},{2,10},{8,16},{10,18},{16,24},{18,26},{24,28},{26,30},{28,20... | collective-permute-start | bytes 786440 | tf_op jit(solution)/shard_map/ppermute | solution.py:478
  12.1 0.2 collective-permute-start.8
  12.3 0.0 collective-permute-done.1
  12.3 2.4 %collective-permute-start.2 = (bf16[16,2048]{1,0:T(8,128)(2,1)S(1)}, bf16[16,2048]{1,0:T(8,128)(2,1)S(1)}, u32[]{:S(2)}, u32[]{:S(2)}) collective-permute-start(bf16[16,2048]{1,0:T(8,128)(2,1)S(1)} %slice_add_fusion), channel_id=1, source_target_pairs={{0,16},{2,18},{4,20},{6,22},{8,24},{10,26},{12,28},{14,30},{16,0},... | collective-permute-start | bytes 196616 | tf_op jit(solution)/shard_map/ppermute | solution.py:424
  14.7 3.4 %collective-permute-done.12.refs_2_ = bf16[64,2048]{1,0:T(8,128)(2,1)S(1)} collective-permute-done((bf16[64,2048]{1,0:T(8,128)(2,1)S(1)}, bf16[64,2048]{1,0:T(8,128)(2,1)S(1)}, u32[]{:S(2)}, u32[]{:S(2)}) %collective-permute-start.12) | collective-permute-done | bytes 262176 | tf_op jit(solution)/shard_map/ppermute | solution.py:478
  18.1 1.3 %collective-permute-start.13 = (bf16[64,2048]{1,0:T(8,128)(2,1)S(1)}, bf16[64,2048]{1,0:T(8,128)(2,1)S(1)}, u32[]{:S(2)}, u32[]{:S(2)}) collective-permute-start(bf16[64,2048]{1,0:T(8,128)(2,1)S(1)} %collective-permute-done.12.refs_2_), channel_id=1, source_target_pairs={{0,8},{2,10},{8,16},{10,18},{16,24},{18,26},{24,28},{26,30},{28,20... | collective-permute-start | bytes 786440 | tf_op jit(solution)/shard_map/ppermute | solution.py:478
  19.3 0.2 convert_reduce_fusion
  19.5 2.0 %collective-permute-done.2 = bf16[16,2048]{1,0:T(8,128)(2,1)S(1)} collective-permute-done((bf16[16,2048]{1,0:T(8,128)(2,1)S(1)}, bf16[16,2048]{1,0:T(8,128)(2,1)S(1)}, u32[]{:S(2)}, u32[]{:S(2)}) %collective-permute-start.2) | collective-permute-done | bytes 65568 | tf_op jit(solution)/shard_map/ppermute | solution.py:424
  21.6 1.0 %collective-permute-start.3 = (bf16[16,2048]{1,0:T(8,128)(2,1)S(1)}, bf16[16,2048]{1,0:T(8,128)(2,1)S(1)}, u32[]{:S(2)}, u32[]{:S(2)}) collective-permute-start(bf16[16,2048]{1,0:T(8,128)(2,1)S(1)} %add.183), channel_id=1, source_target_pairs={{0,8},{2,10},{4,12},{6,14},{8,0},{10,2},{12,4},{14,6},{16,24},{18,... | collective-permute-start | bytes 196616 | tf_op jit(solution)/shard_map/ppermute | solution.py:424
  22.6 2.9 %collective-permute-start.21 = (bf16[64,2048]{1,0:T(8,128)(2,1)S(1)}, bf16[64,2048]{1,0:T(8,128)(2,1)S(1)}, u32[]{:S(2)}, u32[]{:S(2)}) collective-permute-start(bf16[64,2048]{1,0:T(8,128)(2,1)S(1)} %whiten.1.refs_0_), channel_id=1, source_target_pairs={{0,2},{2,0},{4,6},{6,4},{8,10},{10,8},{12,14},{14,12},{16,18},{18,... | collective-permute-start | bytes 786440 | tf_op jit(solution)/shard_map/ppermute | solution.py:424
  25.5 0.0 collective-permute-done.3
  25.5 1.1 %collective-permute-start.4 = (bf16[16,2048]{1,0:T(8,128)(2,1)S(1)}, bf16[16,2048]{1,0:T(8,128)(2,1)S(1)}, u32[]{:S(2)}, u32[]{:S(2)}) collective-permute-start(bf16[16,2048]{1,0:T(8,128)(2,1)S(1)} %add.184.found_ref), channel_id=1, source_target_pairs={{0,4},{2,6},{4,0},{6,2},{8,12},{10,14},{12,8},{14,10},{16,20},{18,... | collective-permute-start | bytes 196616 | tf_op jit(solution)/shard_map/ppermute | solution.py:424
  26.7 0.1 select_reduce_fusion
  26.9 0.1 copy.10.mine_ref
  27.0 0.1 copy.11.sib_ref
  27.0 0.0 collective-permute-done.8.refs_0_
  27.0 0.4 collective-permute-start.9
  27.4 1.3 %collective-permute-done.4.more_ref = bf16[16,2048]{1,0:T(8,128)(2,1)S(1)} collective-permute-done((bf16[16,2048]{1,0:T(8,128)(2,1)S(1)}, bf16[16,2048]{1,0:T(8,128)(2,1)S(1)}, u32[]{:S(2)}, u32[]{:S(2)}) %collective-permute-start.4) | collective-permute-done | bytes 65568 | tf_op jit(solution)/shard_map/ppermute | solution.py:424
  28.7 0.3 pick_slots.1
  29.0 4.7 %collective-permute-start.5 = (bf16[16,2048]{1,0:T(8,128)(2,1)S(1)}, bf16[16,2048]{1,0:T(8,128)(2,1)S(1)}, u32[]{:S(2)}, u32[]{:S(2)}) collective-permute-start(bf16[16,2048]{1,0:T(8,128)(2,1)S(1)} %get-tuple-element.16), channel_id=1, source_target_pairs={{0,2},{2,0},{4,6},{6,4},{8,10},{10,8},{12,14},{14,12},{16,18},{18,... | collective-permute-start | bytes 196616 | tf_op jit(solution)/shard_map/ppermute | solution.py:424
  33.7 0.0 collective-permute-done.13.refs_2_
  33.7 0.9 %collective-permute-start.14 = (bf16[64,2048]{1,0:T(8,128)(2,1)S(1)}, bf16[64,2048]{1,0:T(8,128)(2,1)S(1)}, u32[]{:S(2)}, u32[]{:S(2)}) collective-permute-start(bf16[64,2048]{1,0:T(8,128)(2,1)S(1)} %collective-permute-done.13.refs_2_), channel_id=1, source_target_pairs={{0,8},{2,10},{8,16},{10,18},{16,24},{18,26},{24,28},{26,30},{28,20... | collective-permute-start | bytes 786440 | tf_op jit(solution)/shard_map/ppermute | solution.py:478
  34.6 0.1 pad_add_fusion.5.rows_ref
  34.7 0.4 collective-permute-start.22
  35.1 0.0 collective-permute-done.5
  35.1 0.2 collective-permute-start.19
  35.2 0.1 pad_add_fusion.4.rows_ref
  35.4 0.0 collective-permute-done.21.refs_1_
  35.4 0.9 %collective-permute-start.6 = (bf16[16,2048]{1,0:T(8,128)(2,1)S(1)}, bf16[16,2048]{1,0:T(8,128)(2,1)S(1)}, u32[]{:S(2)}, u32[]{:S(2)}) collective-permute-start(bf16[16,2048]{1,0:T(8,128)(2,1)S(1)} %add.185.own_ref), channel_id=1, source_target_pairs={{0,1},{1,0},{2,3},{3,2},{4,5},{5,4},{6,7},{7,6},{8,9},{9,8},{10,11... | collective-permute-start | bytes 196616 | tf_op jit(solution)/shard_map/ppermute | solution.py:455
  36.3 0.1 pad_add_fusion.3.rows_ref
  36.4 2.5 %collective-permute-done.6.other_ref = bf16[16,2048]{1,0:T(8,128)(2,1)S(1)} collective-permute-done((bf16[16,2048]{1,0:T(8,128)(2,1)S(1)}, bf16[16,2048]{1,0:T(8,128)(2,1)S(1)}, u32[]{:S(2)}, u32[]{:S(2)}) %collective-permute-start.6) | collective-permute-done | bytes 65568 | tf_op jit(solution)/shard_map/ppermute | solution.py:455
  38.9 1.2 %collective-permute-start.20 = (bf16[64,2048]{1,0:T(8,128)(2,1)S(1)}, bf16[64,2048]{1,0:T(8,128)(2,1)S(1)}, u32[]{:S(2)}, u32[]{:S(2)}) collective-permute-start(bf16[64,2048]{1,0:T(8,128)(2,1)S(1)} %collective-permute-done.13.refs_2_), channel_id=1, source_target_pairs={{0,2},{2,0},{4,6},{6,4},{8,10},{10,8},{12,14},{14,12},{16,18},{18,... | collective-permute-start | bytes 786440 | tf_op jit(solution)/shard_map/ppermute | solution.py:424
  40.1 0.0 collective-permute-done.9.refs_0_
  40.1 0.6 collective-permute-start.10
  40.7 0.8 %collective-permute-done.14.refs_2_ = bf16[64,2048]{1,0:T(8,128)(2,1)S(1)} collective-permute-done((bf16[64,2048]{1,0:T(8,128)(2,1)S(1)}, bf16[64,2048]{1,0:T(8,128)(2,1)S(1)}, u32[]{:S(2)}, u32[]{:S(2)}) %collective-permute-start.14) | collective-permute-done | bytes 262176 | tf_op jit(solution)/shard_map/ppermute | solution.py:478
  41.5 0.9 %collective-permute-start.15 = (bf16[64,2048]{1,0:T(8,128)(2,1)S(1)}, bf16[64,2048]{1,0:T(8,128)(2,1)S(1)}, u32[]{:S(2)}, u32[]{:S(2)}) collective-permute-start(bf16[64,2048]{1,0:T(8,128)(2,1)S(1)} %collective-permute-done.14.refs_2_), channel_id=1, source_target_pairs={{0,8},{2,10},{8,16},{10,18},{16,24},{18,26},{24,28},{26,30},{28,20... | collective-permute-start | bytes 786440 | tf_op jit(solution)/shard_map/ppermute | solution.py:478
  42.4 0.1 pad_add_fusion.1.rows_ref
  42.5 2.3 %whiten_sources.1.src_ref = f32[32,2048]{1,0:T(8,128)S(1)} custom-call(bf16[16,2048]{1,0:T(8,128)(2,1)S(1)} %add.185.own_ref, bf16[16,2048]{1,0:T(8,128)(2,1)S(1)} %collective-permute-done.6.other_ref), custom_call_target="tpu_custom_call" | custom-call | flops 134217728 | bytes 4194304 | tf_op jit(solution)/shard_map/whiten_sources/pallas_call | solution.py:259
  44.8 1.3 %collective-permute-start.17 = (bf16[64,2048]{1,0:T(8,128)(2,1)S(1)}, bf16[64,2048]{1,0:T(8,128)(2,1)S(1)}, u32[]{:S(2)}, u32[]{:S(2)}) collective-permute-start(bf16[64,2048]{1,0:T(8,128)(2,1)S(1)} %collective-permute-done.9.refs_0_), channel_id=1, source_target_pairs={{0,2},{2,0},{4,6},{6,4},{8,10},{10,8},{12,14},{14,12},{16,18},{18,... | collective-permute-start | bytes 786440 | tf_op jit(solution)/shard_map/ppermute | solution.py:424
  46.1 0.0 collective-permute-done.19.refs_1_
  46.1 0.1 collective-permute-start.18
  46.2 3.7 %gather_slots.4.refs_4_ = bf16[12,16,32,256]{3,2,1,0:T(8,128)(2,1)} custom-call(s32[4]{0:T(128)S(1)} %pad_add_fusion.5.rows_ref, f32[32,2048]{1,0:T(8,128)S(1)} %whiten_sources.1.src_ref, bf16[2048,256]{1,0:T(8,128)(2,1)S(1)} %get-tuple-element.17.lag_ref, bf16[64,2048]{1,0:T(8,128)(2,1)S(1)} %whiten.1.refs_0_, ...), custom_call_target="tpu_custom_call" | custom-call | flops 1610612736 | bytes 4194304 | tf_op jit(solution)/shard_map/gather_slots/pallas_call | solution.py:374
  49.9 0.0 collective-permute-done.10.refs_0_
  49.9 0.5 collective-permute-start.11
  50.4 0.1 collective-permute-start.16
  50.5 3.6 %gather_slots.5.refs_4_ = bf16[12,16,32,256]{3,2,1,0:T(8,128)(2,1)} custom-call(s32[4]{0:T(128)S(1)} %pad_add_fusion.4.rows_ref, f32[32,2048]{1,0:T(8,128)S(1)} %whiten_sources.1.src_ref, bf16[2048,256]{1,0:T(8,128)(2,1)S(1)} %get-tuple-element.17.lag_ref, bf16[64,2048]{1,0:T(8,128)(2,1)S(1)} %collective-permute-done.8.refs_0_, ...), custom_call_target="tpu_custom_call", output_to_operand_aliasing={{}: (7, {})} | custom-call | flops 1610612736 | bytes 4194304 | tf_op jit(solution)/shard_map/gather_slots/pallas_call | solution.py:374
  54.1 0.0 collective-permute-done.17.refs_1_
  54.1 0.0 collective-permute-done.18.refs_3_
  54.2 3.7 %gather_slots.6.refs_4_ = bf16[12,16,32,256]{3,2,1,0:T(8,128)(2,1)} custom-call(s32[4]{0:T(128)S(1)} %pad_add_fusion.3.rows_ref, f32[32,2048]{1,0:T(8,128)S(1)} %whiten_sources.1.src_ref, bf16[2048,256]{1,0:T(8,128)(2,1)S(1)} %get-tuple-element.17.lag_ref, bf16[64,2048]{1,0:T(8,128)(2,1)S(1)} %collective-permute-done.9.refs_0_, ...), custom_call_target="tpu_custom_call", output_to_operand_aliasing={{}: (7, {})} | custom-call | flops 1610612736 | bytes 4194304 | tf_op jit(solution)/shard_map/gather_slots/pallas_call | solution.py:374
  57.8 0.0 collective-permute-done.11.refs_1_
  57.8 0.0 collective-permute-done.16.refs_3_
  57.9 3.7 %gather_slots.7 = bf16[12,16,32,256]{3,2,1,0:T(8,128)(2,1)} custom-call(s32[4]{0:T(128)S(1)} %pad_add_fusion.1.rows_ref, f32[32,2048]{1,0:T(8,128)S(1)} %whiten_sources.1.src_ref, bf16[2048,256]{1,0:T(8,128)(2,1)S(1)} %get-tuple-element.17.lag_ref, bf16[64,2048]{1,0:T(8,128)(2,1)S(1)} %collective-permute-done.10.refs_0_, ...), custom_call_target="tpu_custom_call", output_to_operand_aliasing={{}: (7, {})} | custom-call | flops 1610612736 | bytes 4194304 | tf_op jit(solution)/shard_map/gather_slots/pallas_call | solution.py:374
  (13 shorter events, 0.1 us)
Async XLA Ops:
  0.0 19.3 %copy-start.1 = (s32[64,1]{0,1:T(1,128)S(1)}, s32[64,1]{0,1:T(1,128)}, u32[]{:S(2)}) copy-start(s32[64,1]{0,1:T(1,128)} %param.7) | copy-start | bytes 772
  0.8 1.0 %copy-start = (bf16[1,64,2048]{2,1,0:T(8,128)(2,1)S(1)}, bf16[1,64,2048]{2,1,0:T(8,128)(2,1)}, u32[]{:S(2)}) copy-start(bf16[1,64,2048]{2,1,0:T(8,128)(2,1)} %param.4) | copy-start | bytes 786436
  2.6 2.8 %collective-permute-start = (bf16[32,2048]{1,0:T(8,128)(2,1)S(1)}, bf16[32,2048]{1,0:T(8,128)(2,1)S(1)}, u32[]{:S(2)}, u32[]{:S(2)}) collective-permute-start(bf16[32,2048]{1,0:T(8,128)(2,1)S(1)} %get-tuple-element.14), channel_id=1, source_target_pairs={{0,2},{2,0},{4,6},{6,4},{8,10},{10,8},{12,14},{14,12},{16,18},{18,... | collective-permute-start | bytes 393224 | tf_op jit(solution)/shard_map/ppermute | solution.py:424
  2.7 6.7 %collective-permute-start.7 = (bf16[32,2048]{1,0:T(8,128)(2,1)S(1)}, bf16[32,2048]{1,0:T(8,128)(2,1)S(1)}, u32[]{:S(2)}, u32[]{:S(2)}) collective-permute-start(bf16[32,2048]{1,0:T(8,128)(2,1)S(1)} %get-tuple-element.19), channel_id=1, source_target_pairs={{0,1},{1,0},{2,3},{3,2},{4,5},{5,4},{6,7},{7,6},{8,9},{9,8},{10,11... | collective-permute-start | bytes 393224 | tf_op jit(solution)/shard_map/ppermute | solution.py:432
  5.5 6.8 %collective-permute-start.1 = (bf16[16,2048]{1,0:T(8,128)(2,1)S(1)}, bf16[16,2048]{1,0:T(8,128)(2,1)S(1)}, u32[]{:S(2)}, u32[]{:S(2)}) collective-permute-start(bf16[16,2048]{1,0:T(8,128)(2,1)S(1)} %slice.9), channel_id=1, source_target_pairs={{0,4},{2,6},{4,0},{6,2},{8,12},{10,14},{12,8},{14,10},{16,20},{18,... | collective-permute-start | bytes 196616 | tf_op jit(solution)/shard_map/ppermute | solution.py:424
  10.8 7.3 %collective-permute-start.12 = (bf16[64,2048]{1,0:T(8,128)(2,1)S(1)}, bf16[64,2048]{1,0:T(8,128)(2,1)S(1)}, u32[]{:S(2)}, u32[]{:S(2)}) collective-permute-start(bf16[64,2048]{1,0:T(8,128)(2,1)S(1)} %whiten.1.refs_0_), channel_id=1, source_target_pairs={{0,8},{2,10},{8,16},{10,18},{16,24},{18,26},{24,28},{26,30},{28,20... | collective-permute-start | bytes 786440 | tf_op jit(solution)/shard_map/ppermute | solution.py:478
  12.1 14.9 %collective-permute-start.8 = (bf16[64,2048]{1,0:T(8,128)(2,1)S(1)}, bf16[64,2048]{1,0:T(8,128)(2,1)S(1)}, u32[]{:S(2)}, u32[]{:S(2)}) collective-permute-start(bf16[64,2048]{1,0:T(8,128)(2,1)S(1)} %whiten.1.refs_0_), channel_id=1, source_target_pairs={{0,4},{2,6},{8,0},{10,2},{16,8},{18,10},{24,16},{26,18},{28,24},{3... | collective-permute-start | bytes 786440 | tf_op jit(solution)/shard_map/ppermute | solution.py:478
  12.3 9.2 %collective-permute-start.2 = (bf16[16,2048]{1,0:T(8,128)(2,1)S(1)}, bf16[16,2048]{1,0:T(8,128)(2,1)S(1)}, u32[]{:S(2)}, u32[]{:S(2)}) collective-permute-start(bf16[16,2048]{1,0:T(8,128)(2,1)S(1)} %slice_add_fusion), channel_id=1, source_target_pairs={{0,16},{2,18},{4,20},{6,22},{8,24},{10,26},{12,28},{14,30},{16,0},... | collective-permute-start | bytes 196616 | tf_op jit(solution)/shard_map/ppermute | solution.py:424
  18.1 15.6 %collective-permute-start.13 = (bf16[64,2048]{1,0:T(8,128)(2,1)S(1)}, bf16[64,2048]{1,0:T(8,128)(2,1)S(1)}, u32[]{:S(2)}, u32[]{:S(2)}) collective-permute-start(bf16[64,2048]{1,0:T(8,128)(2,1)S(1)} %collective-permute-done.12.refs_2_), channel_id=1, source_target_pairs={{0,8},{2,10},{8,16},{10,18},{16,24},{18,26},{24,28},{26,30},{28,20... | collective-permute-start | bytes 786440 | tf_op jit(solution)/shard_map/ppermute | solution.py:478
  21.6 3.9 %collective-permute-start.3 = (bf16[16,2048]{1,0:T(8,128)(2,1)S(1)}, bf16[16,2048]{1,0:T(8,128)(2,1)S(1)}, u32[]{:S(2)}, u32[]{:S(2)}) collective-permute-start(bf16[16,2048]{1,0:T(8,128)(2,1)S(1)} %add.183), channel_id=1, source_target_pairs={{0,8},{2,10},{4,12},{6,14},{8,0},{10,2},{12,4},{14,6},{16,24},{18,... | collective-permute-start | bytes 196616 | tf_op jit(solution)/shard_map/ppermute | solution.py:424
  22.6 12.8 %collective-permute-start.21 = (bf16[64,2048]{1,0:T(8,128)(2,1)S(1)}, bf16[64,2048]{1,0:T(8,128)(2,1)S(1)}, u32[]{:S(2)}, u32[]{:S(2)}) collective-permute-start(bf16[64,2048]{1,0:T(8,128)(2,1)S(1)} %whiten.1.refs_0_), channel_id=1, source_target_pairs={{0,2},{2,0},{4,6},{6,4},{8,10},{10,8},{12,14},{14,12},{16,18},{18,... | collective-permute-start | bytes 786440 | tf_op jit(solution)/shard_map/ppermute | solution.py:424
  25.5 3.2 %collective-permute-start.4 = (bf16[16,2048]{1,0:T(8,128)(2,1)S(1)}, bf16[16,2048]{1,0:T(8,128)(2,1)S(1)}, u32[]{:S(2)}, u32[]{:S(2)}) collective-permute-start(bf16[16,2048]{1,0:T(8,128)(2,1)S(1)} %add.184.found_ref), channel_id=1, source_target_pairs={{0,4},{2,6},{4,0},{6,2},{8,12},{10,14},{12,8},{14,10},{16,20},{18,... | collective-permute-start | bytes 196616 | tf_op jit(solution)/shard_map/ppermute | solution.py:424
  27.0 13.0 %collective-permute-start.9 = (bf16[64,2048]{1,0:T(8,128)(2,1)S(1)}, bf16[64,2048]{1,0:T(8,128)(2,1)S(1)}, u32[]{:S(2)}, u32[]{:S(2)}) collective-permute-start(bf16[64,2048]{1,0:T(8,128)(2,1)S(1)} %collective-permute-done.8.refs_0_), channel_id=1, source_target_pairs={{0,4},{2,6},{8,0},{10,2},{16,8},{18,10},{24,16},{26,18},{28,24},{3... | collective-permute-start | bytes 786440 | tf_op jit(solution)/shard_map/ppermute | solution.py:478
  29.0 6.1 %collective-permute-start.5 = (bf16[16,2048]{1,0:T(8,128)(2,1)S(1)}, bf16[16,2048]{1,0:T(8,128)(2,1)S(1)}, u32[]{:S(2)}, u32[]{:S(2)}) collective-permute-start(bf16[16,2048]{1,0:T(8,128)(2,1)S(1)} %get-tuple-element.16), channel_id=1, source_target_pairs={{0,2},{2,0},{4,6},{6,4},{8,10},{10,8},{12,14},{14,12},{16,18},{18,... | collective-permute-start | bytes 196616 | tf_op jit(solution)/shard_map/ppermute | solution.py:424
  33.7 7.8 %collective-permute-start.14 = (bf16[64,2048]{1,0:T(8,128)(2,1)S(1)}, bf16[64,2048]{1,0:T(8,128)(2,1)S(1)}, u32[]{:S(2)}, u32[]{:S(2)}) collective-permute-start(bf16[64,2048]{1,0:T(8,128)(2,1)S(1)} %collective-permute-done.13.refs_2_), channel_id=1, source_target_pairs={{0,8},{2,10},{8,16},{10,18},{16,24},{18,26},{24,28},{26,30},{28,20... | collective-permute-start | bytes 786440 | tf_op jit(solution)/shard_map/ppermute | solution.py:478
  34.7 10.1 %collective-permute-start.22 = (bf16[64,2048]{1,0:T(8,128)(2,1)S(1)}, bf16[64,2048]{1,0:T(8,128)(2,1)S(1)}, u32[]{:S(2)}, u32[]{:S(2)}) collective-permute-start(bf16[64,2048]{1,0:T(8,128)(2,1)S(1)} %collective-permute-done.12.refs_2_), channel_id=1, source_target_pairs={{0,2},{2,0},{4,6},{6,4},{8,10},{10,8},{12,14},{14,12},{16,18},{18,... | collective-permute-start | bytes 786440 | tf_op jit(solution)/shard_map/ppermute | solution.py:424
  35.1 11.0 %collective-permute-start.19 = (bf16[64,2048]{1,0:T(8,128)(2,1)S(1)}, bf16[64,2048]{1,0:T(8,128)(2,1)S(1)}, u32[]{:S(2)}, u32[]{:S(2)}) collective-permute-start(bf16[64,2048]{1,0:T(8,128)(2,1)S(1)} %collective-permute-done.8.refs_0_), channel_id=1, source_target_pairs={{0,2},{2,0},{4,6},{6,4},{8,10},{10,8},{12,14},{14,12},{16,18},{18,... | collective-permute-start | bytes 786440 | tf_op jit(solution)/shard_map/ppermute | solution.py:424
  35.4 3.5 %collective-permute-start.6 = (bf16[16,2048]{1,0:T(8,128)(2,1)S(1)}, bf16[16,2048]{1,0:T(8,128)(2,1)S(1)}, u32[]{:S(2)}, u32[]{:S(2)}) collective-permute-start(bf16[16,2048]{1,0:T(8,128)(2,1)S(1)} %add.185.own_ref), channel_id=1, source_target_pairs={{0,1},{1,0},{2,3},{3,2},{4,5},{5,4},{6,7},{7,6},{8,9},{9,8},{10,11... | collective-permute-start | bytes 196616 | tf_op jit(solution)/shard_map/ppermute | solution.py:455
  38.9 11.6 %collective-permute-start.20 = (bf16[64,2048]{1,0:T(8,128)(2,1)S(1)}, bf16[64,2048]{1,0:T(8,128)(2,1)S(1)}, u32[]{:S(2)}, u32[]{:S(2)}) collective-permute-start(bf16[64,2048]{1,0:T(8,128)(2,1)S(1)} %collective-permute-done.13.refs_2_), channel_id=1, source_target_pairs={{0,2},{2,0},{4,6},{6,4},{8,10},{10,8},{12,14},{14,12},{16,18},{18,... | collective-permute-start | bytes 786440 | tf_op jit(solution)/shard_map/ppermute | solution.py:424
  40.1 9.8 %collective-permute-start.10 = (bf16[64,2048]{1,0:T(8,128)(2,1)S(1)}, bf16[64,2048]{1,0:T(8,128)(2,1)S(1)}, u32[]{:S(2)}, u32[]{:S(2)}) collective-permute-start(bf16[64,2048]{1,0:T(8,128)(2,1)S(1)} %collective-permute-done.9.refs_0_), channel_id=1, source_target_pairs={{0,4},{2,6},{8,0},{10,2},{16,8},{18,10},{24,16},{26,18},{28,24},{3... | collective-permute-start | bytes 786440 | tf_op jit(solution)/shard_map/ppermute | solution.py:478
  41.5 8.9 %collective-permute-start.15 = (bf16[64,2048]{1,0:T(8,128)(2,1)S(1)}, bf16[64,2048]{1,0:T(8,128)(2,1)S(1)}, u32[]{:S(2)}, u32[]{:S(2)}) collective-permute-start(bf16[64,2048]{1,0:T(8,128)(2,1)S(1)} %collective-permute-done.14.refs_2_), channel_id=1, source_target_pairs={{0,8},{2,10},{8,16},{10,18},{16,24},{18,26},{24,28},{26,30},{28,20... | collective-permute-start | bytes 786440 | tf_op jit(solution)/shard_map/ppermute | solution.py:478
  44.8 9.3 %collective-permute-start.17 = (bf16[64,2048]{1,0:T(8,128)(2,1)S(1)}, bf16[64,2048]{1,0:T(8,128)(2,1)S(1)}, u32[]{:S(2)}, u32[]{:S(2)}) collective-permute-start(bf16[64,2048]{1,0:T(8,128)(2,1)S(1)} %collective-permute-done.9.refs_0_), channel_id=1, source_target_pairs={{0,2},{2,0},{4,6},{6,4},{8,10},{10,8},{12,14},{14,12},{16,18},{18,... | collective-permute-start | bytes 786440 | tf_op jit(solution)/shard_map/ppermute | solution.py:424
  46.1 8.1 %collective-permute-start.18 = (bf16[64,2048]{1,0:T(8,128)(2,1)S(1)}, bf16[64,2048]{1,0:T(8,128)(2,1)S(1)}, u32[]{:S(2)}, u32[]{:S(2)}) collective-permute-start(bf16[64,2048]{1,0:T(8,128)(2,1)S(1)} %collective-permute-done.14.refs_2_), channel_id=1, source_target_pairs={{0,2},{2,0},{4,6},{6,4},{8,10},{10,8},{12,14},{14,12},{16,18},{18,... | collective-permute-start | bytes 786440 | tf_op jit(solution)/shard_map/ppermute | solution.py:424
  49.9 7.9 %collective-permute-start.11 = (bf16[64,2048]{1,0:T(8,128)(2,1)S(1)}, bf16[64,2048]{1,0:T(8,128)(2,1)S(1)}, u32[]{:S(2)}, u32[]{:S(2)}) collective-permute-start(bf16[64,2048]{1,0:T(8,128)(2,1)S(1)} %collective-permute-done.10.refs_0_), channel_id=1, source_target_pairs={{0,2},{2,0},{4,6},{6,4},{8,10},{10,8},{12,14},{14,12},{16,18},{18,... | collective-permute-start | bytes 786440 | tf_op jit(solution)/shard_map/ppermute | solution.py:424
  50.4 7.5 %collective-permute-start.16 = (bf16[64,2048]{1,0:T(8,128)(2,1)S(1)}, bf16[64,2048]{1,0:T(8,128)(2,1)S(1)}, u32[]{:S(2)}, u32[]{:S(2)}) collective-permute-start(bf16[64,2048]{1,0:T(8,128)(2,1)S(1)} %collective-permute-done.15.refs_2_), channel_id=1, source_target_pairs={{0,2},{2,0},{4,6},{6,4},{8,10},{10,8},{12,14},{14,12},{16,18},{18,... | collective-permute-start | bytes 786440 | tf_op jit(solution)/shard_map/ppermute | solution.py:424

commit v2 on v1

--- a/solution.py
+++ b/solution.py
@@ -322,12 +322,14 @@
     for g, first in enumerate(starts):
         slots = list(range(first, min(capacity, first + per)))
         cross = crosses[g % len(crosses)]
-        for n, slot in enumerate(slots):
+        for pair in range(0, len(slots), 2):
+            members = slots[pair : pair + 2]
             for lo in range(0, NF, width):
-                real0, imag0, real1, imag1 = [
+                turned = [
                     jnp.broadcast_to(
                         src_ref[at : at + 1, first_bin : first_bin + width], (16, width)
                     ).astype(bf16)
+                    for slot in members
                     for at in (slot, slot + second)
                     for first_bin in (lo, NF + lo)
                 ]
@@ -338,13 +340,15 @@
                             for at in (top, receivers + top)
                             for first_bin in (lo, NF + lo)
                         ]
-                        row = (n * count + u) * receivers + top
-                        cross[row : row + 16, lo : lo + width] = (
-                            real0 * wr0 + imag0 * wi0 + (real1 * wr1 + imag1 * wi1)
-                        )
-                        cross[row : row + 16, NF + lo : NF + lo + width] = (
-                            imag0 * wr0 - real0 * wi0 + (imag1 * wr1 - real1 * wi1)
-                        )
+                        for m in range(len(members)):
+                            real0, imag0, real1, imag1 = turned[4 * m : 4 * m + 4]
+                            row = ((pair + m) * count + u) * receivers + top
+                            cross[row : row + 16, lo : lo + width] = (
+                                real0 * wr0 + imag0 * wi0 + (real1 * wr1 + imag1 * wi1)
+                            )
+                            cross[row : row + 16, NF + lo : NF + lo + width] = (
+                                imag0 * wr0 - real0 * wi0 + (imag1 * wr1 - real1 * wi1)
+                            )
         filled = len(slots) * count * receivers
         stacked = jnp.dot(cross[:filled, :], lag_ref[...], preferred_element_type=f32)
         mean_sq = jnp.mean(stacked * stacked, axis=-1, keepdims=True)
@@ -366,7 +370,7 @@
 def gather_slots(rows, src, lag, units, held, capacity, row_count):
     count = len(units)
     receivers = units[0].shape[0] // 2
-    per = 4
+    per = max(2, 16 // count)
     steps = -(-capacity // per)
     vmem, anywhere = pl.BlockSpec(memory_space=pltpu.VMEM), pl.BlockSpec(memory_space=pl.ANY)
     prior = () if held is None else (held,)
@@ -485,8 +489,9 @@
         pairs[d] = (held[d], flipped(held[d], 1))
     src = whiten_sources(own_src, other_src)
     out = None
-    for n in range(depth):
-        places = order[2 * n : 2 * n + 2]
+    cuts = list(range(0, 2 * depth + 1, 2))
+    for begin, end in zip(cuts, cuts[1:]):
+        places = order[begin:end]
         rows = jnp.stack(
             [row_at((place + d) % chips) + other for d in places for other in (core, 1 - core)]
         ).astype(jnp.int32)

time: 62.2 us -> 61.7 us (level)
  transfers between devices with their start and end apart: 23 -> 23, of which waited for: 5 -> 5; matrix products, arithmetic and copies ran while one was open for 2% -> 3% of each run, Pallas kernels for 27% -> 27%
where the time goes in v2:
time: 61.7 us; the launch traced here: 61.2 us
  starting transfers between devices  26.4 us (43%)
  Pallas kernels  21 us (34%)
  waiting for transfers between devices  10.1 us (16%)
  other arithmetic  2.13 us (3%)
  local copies, waits for them, and re-layouts  1.13 us (2%)
    ppermute x14, starting transfers between devices, flipped(): return lax.ppermute(value, 'row', [(r, r ^ bit) for r in range(row_count)])  17.3 us
    pallas_call x4, Pallas kernels, gather_slots(): pl.pallas_call(functools.partial(gather_kernel, count=count, per=per), ou...  14.2 us
    ppermute x7, starting transfers between devices, pairs_body(): held[-sign * k] = lax.ppermute(held[-sign * (k - 1)], 'row', moves)  5.49 us
    ppermute x7, waiting for transfers between devices, pairs_body(): held[-sign * k] = lax.ppermute(held[-sign * (k - 1)], 'row', moves)  4.24 us
    ppermute x14, waiting for transfers between devices, flipped(): return lax.ppermute(value, 'row', [(r, r ^ bit) for r in range(row_count)])  3.37 us
    ppermute x1, starting transfers between devices, pairs_body(): other = lax.ppermute(away, 'seg', swap)  2.69 us
    ppermute x1, waiting for transfers between devices, pairs_body(): other_src = lax.ppermute(own_src, 'seg', swap)  2.47 us
    pallas_call x1, Pallas kernels, whiten_sources(): pl.pallas_call(whiten_sources_kernel, out_shape=jax.ShapeDtypeStruct((2 *...  2.34 us
  transfers between devices with their start and end apart: 23, of which 5 were waited for; matrix products, arithmetic and copies ran while one was open for 3% of the time, Pallas kernels for 27%

profile of v2, /device:TPU:1, one launch (start us, length us, event | category | flops | bytes accessed | tf_op | source)
XLA Modules:
  0.0 61.2 jit_solution(3405782336144065431)
XLA Ops:
  0.0 0.7 %pad_add_fusion.facts_ref = s32[2,64]{1,0:T(2,128)S(1)} fusion(s32[1,64]{1,0:T(1,128)} %bitcast.31, s32[1,64]{1,0:T(1,128)} %bitcast.32), kind=kLoop, calls=%fused_computation.12 | loop fusion | flops 128 | bytes 1024 | tf_op jit(solution)/shard_map/stack | solution.py:297
  0.7 0.1 pad_add_fusion.2.at_ref
  0.8 0.9 %copy-done = bf16[1,64,2048]{2,1,0:T(8,128)(2,1)S(1)} copy-done((bf16[1,64,2048]{2,1,0:T(8,128)(2,1)S(1)}, bf16[1,64,2048]{2,1,0:T(8,128)(2,1)}, u32[]{:S(2)}) %copy-start) | copy-done | bytes 262168
  1.7 0.9 %front.1 = (bf16[32,2048]{1,0:T(8,128)(2,1)S(1)}, bf16[32,2048]{1,0:T(8,128)(2,1)S(1)}, bf16[32,2048]{1,0:T(8,128)(2,1)S(1)}, bf16[32,2048]{1,0:T(8,128)(2,1)S(1)}) custom-call(s32[4]{0:T(128)S(1)} %pad_add_fusion.2.at_ref, s32[2,64]{1,0:T(2,128)S(1)} %pad_add_fusion.facts_ref, bf16[64,2048]{1,0:T(8,128)(2,1)S(1)} %bitcast.28), custom_call_target="tpu_custom_call" | custom-call | flops 16777216 | bytes 1048576 | tf_op jit(solution)/shard_map/front/pallas_call | solution.py:302
  2.6 0.1 collective-permute-start
  2.7 2.7 %collective-permute-start.7 = (bf16[32,2048]{1,0:T(8,128)(2,1)S(1)}, bf16[32,2048]{1,0:T(8,128)(2,1)S(1)}, u32[]{:S(2)}, u32[]{:S(2)}) collective-permute-start(bf16[32,2048]{1,0:T(8,128)(2,1)S(1)} %get-tuple-element.19), channel_id=1, source_target_pairs={{0,1},{1,0},{2,3},{3,2},{4,5},{5,4},{6,7},{7,6},{8,9},{9,8},{10,11... | collective-permute-start | bytes 393224 | tf_op jit(solution)/shard_map/ppermute | solution.py:436
  5.4 0.0 collective-permute-done
  5.5 1.3 %collective-permute-start.1 = (bf16[16,2048]{1,0:T(8,128)(2,1)S(1)}, bf16[16,2048]{1,0:T(8,128)(2,1)S(1)}, u32[]{:S(2)}, u32[]{:S(2)}) collective-permute-start(bf16[16,2048]{1,0:T(8,128)(2,1)S(1)} %slice.9), channel_id=1, source_target_pairs={{0,4},{2,6},{4,0},{6,2},{8,12},{10,14},{12,8},{14,10},{16,20},{18,... | collective-permute-start | bytes 196616 | tf_op jit(solution)/shard_map/ppermute | solution.py:428
  6.8 0.7 %broadcast_compare_fusion.1 = (pred[64]{0:T(512)(128)(4,1)S(1)}, pred[64]{0:T(512)(128)(4,1)S(1)}, pred[64]{0:T(512)(128)(4,1)S(1)}) fusion(s32[]{:T(128)} %axis_index.23, s32[64,1]{0,1:T(1,128)} %param.7, s32[]{:T(128)S(6)} %xor.17, s32[]{:T(128)S(6)} %add.180, s32[]{:T(128)S(6)} %mul.75), kind=kLoop, calls=%fused_computation.20 | loop fusion | flops 320 | bytes 464 | tf_op jit(solution)/shard_map/eq | solution.py:452
  7.4 2.0 %tables.1 = (bf16[1024,2048]{1,0:T(8,128)(2,1)S(1)}, bf16[2048,256]{1,0:T(8,128)(2,1)S(1)}) custom-call(), custom_call_target="tpu_custom_call" | custom-call | flops 6291456 | bytes 4194304 | tf_op jit(solution)/shard_map/tables/pallas_call | solution.py:198
  9.4 0.0 collective-permute-done.7.other_ref
  9.5 1.3 %whiten.1.refs_0_ = bf16[64,2048]{1,0:T(8,128)(2,1)S(1)} custom-call(bf16[32,2048]{1,0:T(8,128)(2,1)S(1)} %get-tuple-element.18.own_ref, bf16[32,2048]{1,0:T(8,128)(2,1)S(1)} %collective-permute-done.7.other_ref, bf16[1024,2048]{1,0:T(8,128)(2,1)S(1)} %get-tuple-element.20.dft_ref), custom_call_target="tpu_custom_call" | custom-call | flops 268435456 | bytes 4194304 | tf_op jit(solution)/shard_map/whiten/pallas_call | solution.py:241
  10.8 1.3 %collective-permute-start.12 = (bf16[64,2048]{1,0:T(8,128)(2,1)S(1)}, bf16[64,2048]{1,0:T(8,128)(2,1)S(1)}, u32[]{:S(2)}, u32[]{:S(2)}) collective-permute-start(bf16[64,2048]{1,0:T(8,128)(2,1)S(1)} %whiten.1.refs_0_), channel_id=1, source_target_pairs={{0,8},{2,10},{8,16},{10,18},{16,24},{18,26},{24,28},{26,30},{28,20... | collective-permute-start | bytes 786440 | tf_op jit(solution)/shard_map/ppermute | solution.py:482
  12.1 0.2 collective-permute-start.8
  12.3 0.0 collective-permute-done.1
  12.3 2.4 %collective-permute-start.2 = (bf16[16,2048]{1,0:T(8,128)(2,1)S(1)}, bf16[16,2048]{1,0:T(8,128)(2,1)S(1)}, u32[]{:S(2)}, u32[]{:S(2)}) collective-permute-start(bf16[16,2048]{1,0:T(8,128)(2,1)S(1)} %slice_add_fusion), channel_id=1, source_target_pairs={{0,16},{2,18},{4,20},{6,22},{8,24},{10,26},{12,28},{14,30},{16,0},... | collective-permute-start | bytes 196616 | tf_op jit(solution)/shard_map/ppermute | solution.py:428
  14.7 3.4 %collective-permute-done.12.refs_2_ = bf16[64,2048]{1,0:T(8,128)(2,1)S(1)} collective-permute-done((bf16[64,2048]{1,0:T(8,128)(2,1)S(1)}, bf16[64,2048]{1,0:T(8,128)(2,1)S(1)}, u32[]{:S(2)}, u32[]{:S(2)}) %collective-permute-start.12) | collective-permute-done | bytes 262176 | tf_op jit(solution)/shard_map/ppermute | solution.py:482
  18.1 1.3 %collective-permute-start.13 = (bf16[64,2048]{1,0:T(8,128)(2,1)S(1)}, bf16[64,2048]{1,0:T(8,128)(2,1)S(1)}, u32[]{:S(2)}, u32[]{:S(2)}) collective-permute-start(bf16[64,2048]{1,0:T(8,128)(2,1)S(1)} %collective-permute-done.12.refs_2_), channel_id=1, source_target_pairs={{0,8},{2,10},{8,16},{10,18},{16,24},{18,26},{24,28},{26,30},{28,20... | collective-permute-start | bytes 786440 | tf_op jit(solution)/shard_map/ppermute | solution.py:482
  19.3 0.2 convert_reduce_fusion
  19.5 2.0 %collective-permute-done.2 = bf16[16,2048]{1,0:T(8,128)(2,1)S(1)} collective-permute-done((bf16[16,2048]{1,0:T(8,128)(2,1)S(1)}, bf16[16,2048]{1,0:T(8,128)(2,1)S(1)}, u32[]{:S(2)}, u32[]{:S(2)}) %collective-permute-start.2) | collective-permute-done | bytes 65568 | tf_op jit(solution)/shard_map/ppermute | solution.py:428
  21.6 1.0 %collective-permute-start.3 = (bf16[16,2048]{1,0:T(8,128)(2,1)S(1)}, bf16[16,2048]{1,0:T(8,128)(2,1)S(1)}, u32[]{:S(2)}, u32[]{:S(2)}) collective-permute-start(bf16[16,2048]{1,0:T(8,128)(2,1)S(1)} %add.183), channel_id=1, source_target_pairs={{0,8},{2,10},{4,12},{6,14},{8,0},{10,2},{12,4},{14,6},{16,24},{18,... | collective-permute-start | bytes 196616 | tf_op jit(solution)/shard_map/ppermute | solution.py:428
  22.6 2.9 %collective-permute-start.21 = (bf16[64,2048]{1,0:T(8,128)(2,1)S(1)}, bf16[64,2048]{1,0:T(8,128)(2,1)S(1)}, u32[]{:S(2)}, u32[]{:S(2)}) collective-permute-start(bf16[64,2048]{1,0:T(8,128)(2,1)S(1)} %whiten.1.refs_0_), channel_id=1, source_target_pairs={{0,2},{2,0},{4,6},{6,4},{8,10},{10,8},{12,14},{14,12},{16,18},{18,... | collective-permute-start | bytes 786440 | tf_op jit(solution)/shard_map/ppermute | solution.py:428
  25.5 0.0 collective-permute-done.3
  25.5 1.1 %collective-permute-start.4 = (bf16[16,2048]{1,0:T(8,128)(2,1)S(1)}, bf16[16,2048]{1,0:T(8,128)(2,1)S(1)}, u32[]{:S(2)}, u32[]{:S(2)}) collective-permute-start(bf16[16,2048]{1,0:T(8,128)(2,1)S(1)} %add.184.found_ref), channel_id=1, source_target_pairs={{0,4},{2,6},{4,0},{6,2},{8,12},{10,14},{12,8},{14,10},{16,20},{18,... | collective-permute-start | bytes 196616 | tf_op jit(solution)/shard_map/ppermute | solution.py:428
  26.7 0.1 select_reduce_fusion
  26.9 0.1 copy.10.mine_ref
  27.0 0.1 copy.11.sib_ref
  27.0 0.0 collective-permute-done.8.refs_0_
  27.0 0.4 collective-permute-start.9
  27.4 1.3 %collective-permute-done.4.more_ref = bf16[16,2048]{1,0:T(8,128)(2,1)S(1)} collective-permute-done((bf16[16,2048]{1,0:T(8,128)(2,1)S(1)}, bf16[16,2048]{1,0:T(8,128)(2,1)S(1)}, u32[]{:S(2)}, u32[]{:S(2)}) %collective-permute-start.4) | collective-permute-done | bytes 65568 | tf_op jit(solution)/shard_map/ppermute | solution.py:428
  28.7 0.3 pick_slots.1
  29.0 4.7 %collective-permute-start.5 = (bf16[16,2048]{1,0:T(8,128)(2,1)S(1)}, bf16[16,2048]{1,0:T(8,128)(2,1)S(1)}, u32[]{:S(2)}, u32[]{:S(2)}) collective-permute-start(bf16[16,2048]{1,0:T(8,128)(2,1)S(1)} %get-tuple-element.16), channel_id=1, source_target_pairs={{0,2},{2,0},{4,6},{6,4},{8,10},{10,8},{12,14},{14,12},{16,18},{18,... | collective-permute-start | bytes 196616 | tf_op jit(solution)/shard_map/ppermute | solution.py:428
  33.7 0.0 collective-permute-done.13.refs_2_
  33.7 0.9 %collective-permute-start.14 = (bf16[64,2048]{1,0:T(8,128)(2,1)S(1)}, bf16[64,2048]{1,0:T(8,128)(2,1)S(1)}, u32[]{:S(2)}, u32[]{:S(2)}) collective-permute-start(bf16[64,2048]{1,0:T(8,128)(2,1)S(1)} %collective-permute-done.13.refs_2_), channel_id=1, source_target_pairs={{0,8},{2,10},{8,16},{10,18},{16,24},{18,26},{24,28},{26,30},{28,20... | collective-permute-start | bytes 786440 | tf_op jit(solution)/shard_map/ppermute | solution.py:482
  34.6 0.1 pad_add_fusion.5.rows_ref
  34.7 0.4 collective-permute-start.22
  35.1 0.0 collective-permute-done.5
  35.1 0.2 collective-permute-start.19
  35.2 0.1 pad_add_fusion.4.rows_ref
  35.4 0.0 collective-permute-done.21.refs_1_
  35.4 0.9 %collective-permute-start.6 = (bf16[16,2048]{1,0:T(8,128)(2,1)S(1)}, bf16[16,2048]{1,0:T(8,128)(2,1)S(1)}, u32[]{:S(2)}, u32[]{:S(2)}) collective-permute-start(bf16[16,2048]{1,0:T(8,128)(2,1)S(1)} %add.185.own_ref), channel_id=1, source_target_pairs={{0,1},{1,0},{2,3},{3,2},{4,5},{5,4},{6,7},{7,6},{8,9},{9,8},{10,11... | collective-permute-start | bytes 196616 | tf_op jit(solution)/shard_map/ppermute | solution.py:459
  36.3 0.1 pad_add_fusion.3.rows_ref
  36.4 2.5 %collective-permute-done.6.other_ref = bf16[16,2048]{1,0:T(8,128)(2,1)S(1)} collective-permute-done((bf16[16,2048]{1,0:T(8,128)(2,1)S(1)}, bf16[16,2048]{1,0:T(8,128)(2,1)S(1)}, u32[]{:S(2)}, u32[]{:S(2)}) %collective-permute-start.6) | collective-permute-done | bytes 65568 | tf_op jit(solution)/shard_map/ppermute | solution.py:459
  38.9 1.2 %collective-permute-start.20 = (bf16[64,2048]{1,0:T(8,128)(2,1)S(1)}, bf16[64,2048]{1,0:T(8,128)(2,1)S(1)}, u32[]{:S(2)}, u32[]{:S(2)}) collective-permute-start(bf16[64,2048]{1,0:T(8,128)(2,1)S(1)} %collective-permute-done.13.refs_2_), channel_id=1, source_target_pairs={{0,2},{2,0},{4,6},{6,4},{8,10},{10,8},{12,14},{14,12},{16,18},{18,... | collective-permute-start | bytes 786440 | tf_op jit(solution)/shard_map/ppermute | solution.py:428
  40.1 0.0 collective-permute-done.9.refs_0_
  40.1 0.6 collective-permute-start.10
  40.7 0.8 %collective-permute-done.14.refs_2_ = bf16[64,2048]{1,0:T(8,128)(2,1)S(1)} collective-permute-done((bf16[64,2048]{1,0:T(8,128)(2,1)S(1)}, bf16[64,2048]{1,0:T(8,128)(2,1)S(1)}, u32[]{:S(2)}, u32[]{:S(2)}) %collective-permute-start.14) | collective-permute-done | bytes 262176 | tf_op jit(solution)/shard_map/ppermute | solution.py:482
  41.5 0.9 %collective-permute-start.15 = (bf16[64,2048]{1,0:T(8,128)(2,1)S(1)}, bf16[64,2048]{1,0:T(8,128)(2,1)S(1)}, u32[]{:S(2)}, u32[]{:S(2)}) collective-permute-start(bf16[64,2048]{1,0:T(8,128)(2,1)S(1)} %collective-permute-done.14.refs_2_), channel_id=1, source_target_pairs={{0,8},{2,10},{8,16},{10,18},{16,24},{18,26},{24,28},{26,30},{28,20... | collective-permute-start | bytes 786440 | tf_op jit(solution)/shard_map/ppermute | solution.py:482
  42.4 0.1 pad_add_fusion.1.rows_ref
  42.5 2.3 %whiten_sources.1.src_ref = f32[32,2048]{1,0:T(8,128)S(1)} custom-call(bf16[16,2048]{1,0:T(8,128)(2,1)S(1)} %add.185.own_ref, bf16[16,2048]{1,0:T(8,128)(2,1)S(1)} %collective-permute-done.6.other_ref), custom_call_target="tpu_custom_call" | custom-call | flops 134217728 | bytes 4194304 | tf_op jit(solution)/shard_map/whiten_sources/pallas_call | solution.py:259
  44.8 0.0 collective-permute-done.22.refs_3_
  44.8 1.3 %collective-permute-start.17 = (bf16[64,2048]{1,0:T(8,128)(2,1)S(1)}, bf16[64,2048]{1,0:T(8,128)(2,1)S(1)}, u32[]{:S(2)}, u32[]{:S(2)}) collective-permute-start(bf16[64,2048]{1,0:T(8,128)(2,1)S(1)} %collective-permute-done.9.refs_0_), channel_id=1, source_target_pairs={{0,2},{2,0},{4,6},{6,4},{8,10},{10,8},{12,14},{14,12},{16,18},{18,... | collective-permute-start | bytes 786440 | tf_op jit(solution)/shard_map/ppermute | solution.py:428
  46.1 0.0 collective-permute-done.19.refs_1_
  46.1 0.1 collective-permute-start.18
  46.2 3.6 %gather_slots.4.refs_4_ = bf16[12,16,32,256]{3,2,1,0:T(8,128)(2,1)} custom-call(s32[4]{0:T(128)S(1)} %pad_add_fusion.5.rows_ref, f32[32,2048]{1,0:T(8,128)S(1)} %whiten_sources.1.src_ref, bf16[2048,256]{1,0:T(8,128)(2,1)S(1)} %get-tuple-element.17.lag_ref, bf16[64,2048]{1,0:T(8,128)(2,1)S(1)} %whiten.1.refs_0_, ...), custom_call_target="tpu_custom_call" | custom-call | flops 1610612736 | bytes 4194304 | tf_op jit(solution)/shard_map/gather_slots/pallas_call | solution.py:378
  49.8 0.0 collective-permute-done.10.refs_0_
  49.8 0.5 collective-permute-start.11
  50.3 0.0 collective-permute-done.15.refs_2_
  50.3 0.1 collective-permute-start.16
  50.4 3.5 %gather_slots.5.refs_4_ = bf16[12,16,32,256]{3,2,1,0:T(8,128)(2,1)} custom-call(s32[4]{0:T(128)S(1)} %pad_add_fusion.4.rows_ref, f32[32,2048]{1,0:T(8,128)S(1)} %whiten_sources.1.src_ref, bf16[2048,256]{1,0:T(8,128)(2,1)S(1)} %get-tuple-element.17.lag_ref, bf16[64,2048]{1,0:T(8,128)(2,1)S(1)} %collective-permute-done.8.refs_0_, ...), custom_call_target="tpu_custom_call", output_to_operand_aliasing={{}: (7, {})} | custom-call | flops 1610612736 | bytes 4194304 | tf_op jit(solution)/shard_map/gather_slots/pallas_call | solution.py:378
  53.9 0.0 collective-permute-done.17.refs_1_
  53.9 0.0 collective-permute-done.18.refs_3_
  53.9 3.5 %gather_slots.6.refs_4_ = bf16[12,16,32,256]{3,2,1,0:T(8,128)(2,1)} custom-call(s32[4]{0:T(128)S(1)} %pad_add_fusion.3.rows_ref, f32[32,2048]{1,0:T(8,128)S(1)} %whiten_sources.1.src_ref, bf16[2048,256]{1,0:T(8,128)(2,1)S(1)} %get-tuple-element.17.lag_ref, bf16[64,2048]{1,0:T(8,128)(2,1)S(1)} %collective-permute-done.9.refs_0_, ...), custom_call_target="tpu_custom_call", output_to_operand_aliasing={{}: (7, {})} | custom-call | flops 1610612736 | bytes 4194304 | tf_op jit(solution)/shard_map/gather_slots/pallas_call | solution.py:378
  57.5 3.5 %gather_slots.7 = bf16[12,16,32,256]{3,2,1,0:T(8,128)(2,1)} custom-call(s32[4]{0:T(128)S(1)} %pad_add_fusion.1.rows_ref, f32[32,2048]{1,0:T(8,128)S(1)} %whiten_sources.1.src_ref, bf16[2048,256]{1,0:T(8,128)(2,1)S(1)} %get-tuple-element.17.lag_ref, bf16[64,2048]{1,0:T(8,128)(2,1)S(1)} %collective-permute-done.10.refs_0_, ...), custom_call_target="tpu_custom_call", output_to_operand_aliasing={{}: (7, {})} | custom-call | flops 1610612736 | bytes 4194304 | tf_op jit(solution)/shard_map/gather_slots/pallas_call | solution.py:378
  (13 shorter events, 0.1 us)
Async XLA Ops:
  0.0 19.3 %copy-start.1 = (s32[64,1]{0,1:T(1,128)S(1)}, s32[64,1]{0,1:T(1,128)}, u32[]{:S(2)}) copy-start(s32[64,1]{0,1:T(1,128)} %param.7) | copy-start | bytes 772
  0.8 1.0 %copy-start = (bf16[1,64,2048]{2,1,0:T(8,128)(2,1)S(1)}, bf16[1,64,2048]{2,1,0:T(8,128)(2,1)}, u32[]{:S(2)}) copy-start(bf16[1,64,2048]{2,1,0:T(8,128)(2,1)} %param.4) | copy-start | bytes 786436
  2.6 2.8 %collective-permute-start = (bf16[32,2048]{1,0:T(8,128)(2,1)S(1)}, bf16[32,2048]{1,0:T(8,128)(2,1)S(1)}, u32[]{:S(2)}, u32[]{:S(2)}) collective-permute-start(bf16[32,2048]{1,0:T(8,128)(2,1)S(1)} %get-tuple-element.14), channel_id=1, source_target_pairs={{0,2},{2,0},{4,6},{6,4},{8,10},{10,8},{12,14},{14,12},{16,18},{18,... | collective-permute-start | bytes 393224 | tf_op jit(solution)/shard_map/ppermute | solution.py:428
  2.7 6.7 %collective-permute-start.7 = (bf16[32,2048]{1,0:T(8,128)(2,1)S(1)}, bf16[32,2048]{1,0:T(8,128)(2,1)S(1)}, u32[]{:S(2)}, u32[]{:S(2)}) collective-permute-start(bf16[32,2048]{1,0:T(8,128)(2,1)S(1)} %get-tuple-element.19), channel_id=1, source_target_pairs={{0,1},{1,0},{2,3},{3,2},{4,5},{5,4},{6,7},{7,6},{8,9},{9,8},{10,11... | collective-permute-start | bytes 393224 | tf_op jit(solution)/shard_map/ppermute | solution.py:436
  5.5 6.8 %collective-permute-start.1 = (bf16[16,2048]{1,0:T(8,128)(2,1)S(1)}, bf16[16,2048]{1,0:T(8,128)(2,1)S(1)}, u32[]{:S(2)}, u32[]{:S(2)}) collective-permute-start(bf16[16,2048]{1,0:T(8,128)(2,1)S(1)} %slice.9), channel_id=1, source_target_pairs={{0,4},{2,6},{4,0},{6,2},{8,12},{10,14},{12,8},{14,10},{16,20},{18,... | collective-permute-start | bytes 196616 | tf_op jit(solution)/shard_map/ppermute | solution.py:428
  10.8 7.3 %collective-permute-start.12 = (bf16[64,2048]{1,0:T(8,128)(2,1)S(1)}, bf16[64,2048]{1,0:T(8,128)(2,1)S(1)}, u32[]{:S(2)}, u32[]{:S(2)}) collective-permute-start(bf16[64,2048]{1,0:T(8,128)(2,1)S(1)} %whiten.1.refs_0_), channel_id=1, source_target_pairs={{0,8},{2,10},{8,16},{10,18},{16,24},{18,26},{24,28},{26,30},{28,20... | collective-permute-start | bytes 786440 | tf_op jit(solution)/shard_map/ppermute | solution.py:482
  12.1 14.9 %collective-permute-start.8 = (bf16[64,2048]{1,0:T(8,128)(2,1)S(1)}, bf16[64,2048]{1,0:T(8,128)(2,1)S(1)}, u32[]{:S(2)}, u32[]{:S(2)}) collective-permute-start(bf16[64,2048]{1,0:T(8,128)(2,1)S(1)} %whiten.1.refs_0_), channel_id=1, source_target_pairs={{0,4},{2,6},{8,0},{10,2},{16,8},{18,10},{24,16},{26,18},{28,24},{3... | collective-permute-start | bytes 786440 | tf_op jit(solution)/shard_map/ppermute | solution.py:482
  12.3 9.2 %collective-permute-start.2 = (bf16[16,2048]{1,0:T(8,128)(2,1)S(1)}, bf16[16,2048]{1,0:T(8,128)(2,1)S(1)}, u32[]{:S(2)}, u32[]{:S(2)}) collective-permute-start(bf16[16,2048]{1,0:T(8,128)(2,1)S(1)} %slice_add_fusion), channel_id=1, source_target_pairs={{0,16},{2,18},{4,20},{6,22},{8,24},{10,26},{12,28},{14,30},{16,0},... | collective-permute-start | bytes 196616 | tf_op jit(solution)/shard_map/ppermute | solution.py:428
  18.1 15.6 %collective-permute-start.13 = (bf16[64,2048]{1,0:T(8,128)(2,1)S(1)}, bf16[64,2048]{1,0:T(8,128)(2,1)S(1)}, u32[]{:S(2)}, u32[]{:S(2)}) collective-permute-start(bf16[64,2048]{1,0:T(8,128)(2,1)S(1)} %collective-permute-done.12.refs_2_), channel_id=1, source_target_pairs={{0,8},{2,10},{8,16},{10,18},{16,24},{18,26},{24,28},{26,30},{28,20... | collective-permute-start | bytes 786440 | tf_op jit(solution)/shard_map/ppermute | solution.py:482
  21.6 3.9 %collective-permute-start.3 = (bf16[16,2048]{1,0:T(8,128)(2,1)S(1)}, bf16[16,2048]{1,0:T(8,128)(2,1)S(1)}, u32[]{:S(2)}, u32[]{:S(2)}) collective-permute-start(bf16[16,2048]{1,0:T(8,128)(2,1)S(1)} %add.183), channel_id=1, source_target_pairs={{0,8},{2,10},{4,12},{6,14},{8,0},{10,2},{12,4},{14,6},{16,24},{18,... | collective-permute-start | bytes 196616 | tf_op jit(solution)/shard_map/ppermute | solution.py:428
  22.6 12.8 %collective-permute-start.21 = (bf16[64,2048]{1,0:T(8,128)(2,1)S(1)}, bf16[64,2048]{1,0:T(8,128)(2,1)S(1)}, u32[]{:S(2)}, u32[]{:S(2)}) collective-permute-start(bf16[64,2048]{1,0:T(8,128)(2,1)S(1)} %whiten.1.refs_0_), channel_id=1, source_target_pairs={{0,2},{2,0},{4,6},{6,4},{8,10},{10,8},{12,14},{14,12},{16,18},{18,... | collective-permute-start | bytes 786440 | tf_op jit(solution)/shard_map/ppermute | solution.py:428
  25.5 3.2 %collective-permute-start.4 = (bf16[16,2048]{1,0:T(8,128)(2,1)S(1)}, bf16[16,2048]{1,0:T(8,128)(2,1)S(1)}, u32[]{:S(2)}, u32[]{:S(2)}) collective-permute-start(bf16[16,2048]{1,0:T(8,128)(2,1)S(1)} %add.184.found_ref), channel_id=1, source_target_pairs={{0,4},{2,6},{4,0},{6,2},{8,12},{10,14},{12,8},{14,10},{16,20},{18,... | collective-permute-start | bytes 196616 | tf_op jit(solution)/shard_map/ppermute | solution.py:428
  27.0 13.0 %collective-permute-start.9 = (bf16[64,2048]{1,0:T(8,128)(2,1)S(1)}, bf16[64,2048]{1,0:T(8,128)(2,1)S(1)}, u32[]{:S(2)}, u32[]{:S(2)}) collective-permute-start(bf16[64,2048]{1,0:T(8,128)(2,1)S(1)} %collective-permute-done.8.refs_0_), channel_id=1, source_target_pairs={{0,4},{2,6},{8,0},{10,2},{16,8},{18,10},{24,16},{26,18},{28,24},{3... | collective-permute-start | bytes 786440 | tf_op jit(solution)/shard_map/ppermute | solution.py:482
  29.0 6.1 %collective-permute-start.5 = (bf16[16,2048]{1,0:T(8,128)(2,1)S(1)}, bf16[16,2048]{1,0:T(8,128)(2,1)S(1)}, u32[]{:S(2)}, u32[]{:S(2)}) collective-permute-start(bf16[16,2048]{1,0:T(8,128)(2,1)S(1)} %get-tuple-element.16), channel_id=1, source_target_pairs={{0,2},{2,0},{4,6},{6,4},{8,10},{10,8},{12,14},{14,12},{16,18},{18,... | collective-permute-start | bytes 196616 | tf_op jit(solution)/shard_map/ppermute | solution.py:428
  33.7 7.8 %collective-permute-start.14 = (bf16[64,2048]{1,0:T(8,128)(2,1)S(1)}, bf16[64,2048]{1,0:T(8,128)(2,1)S(1)}, u32[]{:S(2)}, u32[]{:S(2)}) collective-permute-start(bf16[64,2048]{1,0:T(8,128)(2,1)S(1)} %collective-permute-done.13.refs_2_), channel_id=1, source_target_pairs={{0,8},{2,10},{8,16},{10,18},{16,24},{18,26},{24,28},{26,30},{28,20... | collective-permute-start | bytes 786440 | tf_op jit(solution)/shard_map/ppermute | solution.py:482
  34.7 10.1 %collective-permute-start.22 = (bf16[64,2048]{1,0:T(8,128)(2,1)S(1)}, bf16[64,2048]{1,0:T(8,128)(2,1)S(1)}, u32[]{:S(2)}, u32[]{:S(2)}) collective-permute-start(bf16[64,2048]{1,0:T(8,128)(2,1)S(1)} %collective-permute-done.12.refs_2_), channel_id=1, source_target_pairs={{0,2},{2,0},{4,6},{6,4},{8,10},{10,8},{12,14},{14,12},{16,18},{18,... | collective-permute-start | bytes 786440 | tf_op jit(solution)/shard_map/ppermute | solution.py:428
  35.1 11.0 %collective-permute-start.19 = (bf16[64,2048]{1,0:T(8,128)(2,1)S(1)}, bf16[64,2048]{1,0:T(8,128)(2,1)S(1)}, u32[]{:S(2)}, u32[]{:S(2)}) collective-permute-start(bf16[64,2048]{1,0:T(8,128)(2,1)S(1)} %collective-permute-done.8.refs_0_), channel_id=1, source_target_pairs={{0,2},{2,0},{4,6},{6,4},{8,10},{10,8},{12,14},{14,12},{16,18},{18,... | collective-permute-start | bytes 786440 | tf_op jit(solution)/shard_map/ppermute | solution.py:428
  35.4 3.5 %collective-permute-start.6 = (bf16[16,2048]{1,0:T(8,128)(2,1)S(1)}, bf16[16,2048]{1,0:T(8,128)(2,1)S(1)}, u32[]{:S(2)}, u32[]{:S(2)}) collective-permute-start(bf16[16,2048]{1,0:T(8,128)(2,1)S(1)} %add.185.own_ref), channel_id=1, source_target_pairs={{0,1},{1,0},{2,3},{3,2},{4,5},{5,4},{6,7},{7,6},{8,9},{9,8},{10,11... | collective-permute-start | bytes 196616 | tf_op jit(solution)/shard_map/ppermute | solution.py:459
  38.9 11.5 %collective-permute-start.20 = (bf16[64,2048]{1,0:T(8,128)(2,1)S(1)}, bf16[64,2048]{1,0:T(8,128)(2,1)S(1)}, u32[]{:S(2)}, u32[]{:S(2)}) collective-permute-start(bf16[64,2048]{1,0:T(8,128)(2,1)S(1)} %collective-permute-done.13.refs_2_), channel_id=1, source_target_pairs={{0,2},{2,0},{4,6},{6,4},{8,10},{10,8},{12,14},{14,12},{16,18},{18,... | collective-permute-start | bytes 786440 | tf_op jit(solution)/shard_map/ppermute | solution.py:428
  40.1 9.7 %collective-permute-start.10 = (bf16[64,2048]{1,0:T(8,128)(2,1)S(1)}, bf16[64,2048]{1,0:T(8,128)(2,1)S(1)}, u32[]{:S(2)}, u32[]{:S(2)}) collective-permute-start(bf16[64,2048]{1,0:T(8,128)(2,1)S(1)} %collective-permute-done.9.refs_0_), channel_id=1, source_target_pairs={{0,4},{2,6},{8,0},{10,2},{16,8},{18,10},{24,16},{26,18},{28,24},{3... | collective-permute-start | bytes 786440 | tf_op jit(solution)/shard_map/ppermute | solution.py:482
  41.5 8.7 %collective-permute-start.15 = (bf16[64,2048]{1,0:T(8,128)(2,1)S(1)}, bf16[64,2048]{1,0:T(8,128)(2,1)S(1)}, u32[]{:S(2)}, u32[]{:S(2)}) collective-permute-start(bf16[64,2048]{1,0:T(8,128)(2,1)S(1)} %collective-permute-done.14.refs_2_), channel_id=1, source_target_pairs={{0,8},{2,10},{8,16},{10,18},{16,24},{18,26},{24,28},{26,30},{28,20... | collective-permute-start | bytes 786440 | tf_op jit(solution)/shard_map/ppermute | solution.py:482
  44.8 9.1 %collective-permute-start.17 = (bf16[64,2048]{1,0:T(8,128)(2,1)S(1)}, bf16[64,2048]{1,0:T(8,128)(2,1)S(1)}, u32[]{:S(2)}, u32[]{:S(2)}) collective-permute-start(bf16[64,2048]{1,0:T(8,128)(2,1)S(1)} %collective-permute-done.9.refs_0_), channel_id=1, source_target_pairs={{0,2},{2,0},{4,6},{6,4},{8,10},{10,8},{12,14},{14,12},{16,18},{18,... | collective-permute-start | bytes 786440 | tf_op jit(solution)/shard_map/ppermute | solution.py:428
  46.1 7.8 %collective-permute-start.18 = (bf16[64,2048]{1,0:T(8,128)(2,1)S(1)}, bf16[64,2048]{1,0:T(8,128)(2,1)S(1)}, u32[]{:S(2)}, u32[]{:S(2)}) collective-permute-start(bf16[64,2048]{1,0:T(8,128)(2,1)S(1)} %collective-permute-done.14.refs_2_), channel_id=1, source_target_pairs={{0,2},{2,0},{4,6},{6,4},{8,10},{10,8},{12,14},{14,12},{16,18},{18,... | collective-permute-start | bytes 786440 | tf_op jit(solution)/shard_map/ppermute | solution.py:428
  49.8 7.7 %collective-permute-start.11 = (bf16[64,2048]{1,0:T(8,128)(2,1)S(1)}, bf16[64,2048]{1,0:T(8,128)(2,1)S(1)}, u32[]{:S(2)}, u32[]{:S(2)}) collective-permute-start(bf16[64,2048]{1,0:T(8,128)(2,1)S(1)} %collective-permute-done.10.refs_0_), channel_id=1, source_target_pairs={{0,2},{2,0},{4,6},{6,4},{8,10},{10,8},{12,14},{14,12},{16,18},{18,... | collective-permute-start | bytes 786440 | tf_op jit(solution)/shard_map/ppermute | solution.py:428
  50.3 7.2 %collective-permute-start.16 = (bf16[64,2048]{1,0:T(8,128)(2,1)S(1)}, bf16[64,2048]{1,0:T(8,128)(2,1)S(1)}, u32[]{:S(2)}, u32[]{:S(2)}) collective-permute-start(bf16[64,2048]{1,0:T(8,128)(2,1)S(1)} %collective-permute-done.15.refs_2_), channel_id=1, source_target_pairs={{0,2},{2,0},{4,6},{6,4},{8,10},{10,8},{12,14},{14,12},{16,18},{18,... | collective-permute-start | bytes 786440 | tf_op jit(solution)/shard_map/ppermute | solution.py:428
